TPU v7x, 32 devices: a whole 2x2x4 slice. The times are simulated.
32 devices in a mesh: dp: 8 (over z, x), tensor: 4 (over y, core).
Axes of the slice: x: 2, y: 2, z: 4, core: 2. Of those that a mesh axis runs over, the one named last changes fastest.
Arguments:
- images: bfloat16 [64, 576, 768], P(('dp', 'tensor')), may hold values from -6 to 6
- keep_mask: int32 [64, 576], P(('dp', 'tensor')), may hold values from 0 to 1, as said below
- ln1_gain: float32 [768], replicated, may hold values from 0.25 to 1.75
- ln1_bias: float32 [768], replicated, may hold values from -1.75 to 1.75
- qkv_weight: bfloat16 [768, 2304], replicated, may hold values from -0.3125 to 0.3125
- qkv_bias: float32 [2304], replicated, may hold values from -1.75 to 1.75
- frequencies: float32 [2, 12, 32], replicated, may hold values from -1 to 1
- proj_weight: bfloat16 [768, 768], replicated, may hold values from -1.75 to 1.75
- proj_bias: float32 [768], replicated, may hold values from -1.75 to 1.75
- ln2_gain: float32 [768], replicated, may hold values from 0.25 to 1.75
- ln2_bias: float32 [768], replicated, may hold values from -1.75 to 1.75
- fc1_weight: bfloat16 [768, 3072], P(None, 'tensor'), may hold values from -0.21875 to 0.21875
- fc1_bias: bfloat16 [3072], P('tensor'), may hold values from -1.75 to 1.75
- fc2_weight: bfloat16 [3072, 768], P('tensor'), may hold values from -0.109375 to 0.109375
- fc2_bias: float32 [768], replicated, may hold values from -1.75 to 1.75
- out_grad: bfloat16 [64, 576, 768], P(('dp', 'tensor')), may hold values from -6 to 6
Outputs:
- block_out: bfloat16 [64, 576, 768], P(('dp', 'tensor'))
- input_grad: bfloat16 [64, 576, 768], P(('dp', 'tensor'))
- ln1_gain_grad: float32 [768], replicated
- ln1_bias_grad: float32 [768], replicated
- qkv_weight_grad: float32 [768, 2304], replicated
- qkv_bias_grad: float32 [2304], replicated
- freq_grad: float32 [2, 12, 32], replicated
- proj_weight_grad: float32 [768, 768], replicated
- proj_bias_grad: float32 [768], replicated
- ln2_gain_grad: float32 [768], replicated
- ln2_bias_grad: float32 [768], replicated
- fc1_weight_grad: float32 [768, 3072], P(None, 'tensor')
- fc1_bias_grad: float32 [3072], P('tensor')
- fc2_weight_grad: float32 [3072, 768], P('tensor')
- fc2_bias_grad: float32 [768], replicated
- freq_norm: float32 [], replicated
- rest_norm: float32 [], replicated
Inputs may be any that keep to these rules, and one draw needn't show every extreme that they name: `keep_mask`: every image keeps at least 96 of its 576 slots; the number kept varies widely from image to image.
All inputs are finite; a program needn't handle non-finite values.
Results may differ from a plain program's by a relative error of at most 0.015.
The roundings to bfloat16 on the way count: a program that leaves them out, or rounds other values in their place, can miss the bound.
Values may be sent and summed in bfloat16 or wider, within the bound.
No kernel may reach another device: no remote copies, remote signals or barrier semaphores. Data moves between devices by JAX's collectives and lax.ppermute only.
A program may use at most 192 MiB of HBM per device.

v0:
```python
import math

import jax
import jax.numpy as jnp
from jax import lax
from jax.sharding import PartitionSpec as P

GRID = 24


EPSILON = 1e-06
MASKED_SCORE = -1e30
ROOT_HALF = 0.7071067811865476
DENSITY_SCALE = 0.3989422804014327


def normalize(row_data):
    row_mean = jnp.mean(row_data, axis=-1, keepdims=True)
    centred = row_data - row_mean
    inverse = lax.rsqrt(jnp.mean(centred * centred, axis=-1, keepdims=True) + EPSILON)
    return (centred * inverse, inverse)


def norm_back(grad_unit, unit_rows, inverse):
    return inverse * (
        grad_unit
        - jnp.mean(grad_unit, axis=-1, keepdims=True)
        - unit_rows * jnp.mean(grad_unit * unit_rows, axis=-1, keepdims=True)
    )


def rotate(tensor, cosine, sine):
    half_size = tensor.shape[-1] // 2
    first_half = tensor[..., :half_size]
    second_half = tensor[..., half_size:]
    return jnp.concatenate(
        [first_half * cosine - second_half * sine, first_half * sine + second_half * cosine],
        axis=-1,
    )


def rotate_back(grad_turned, cosine, sine):
    half_size = grad_turned.shape[-1] // 2
    first_half = grad_turned[..., :half_size]
    second_half = grad_turned[..., half_size:]
    return jnp.concatenate(
        [first_half * cosine + second_half * sine, second_half * cosine - first_half * sine],
        axis=-1,
    )


def angle_part(grad_turned, turned):
    half_size = turned.shape[-1] // 2
    return (
        grad_turned[..., half_size:] * turned[..., :half_size]
        - grad_turned[..., :half_size] * turned[..., half_size:]
    )


def gelu_exact(values):
    return 0.5 * values * (1.0 + lax.erf(values * ROOT_HALF))


def gelu_slope(values):
    return (
        0.5 * (1.0 + lax.erf(values * ROOT_HALF))
        + values * jnp.exp(-0.5 * values * values) * DENSITY_SCALE
    )


def contract_rows(left, right):
    return lax.dot_general(
        left, right, (((0,), (0,)), ((), ())), preferred_element_type=jnp.float32
    )


def contract_cols(left, right):
    return lax.dot_general(
        left, right, (((1,), (1,)), ((), ())), preferred_element_type=jnp.float32
    )


def body(
    images,
    keep_mask,
    ln1_gain,
    ln1_bias,
    qkv_weight,
    qkv_bias,
    frequencies,
    proj_weight,
    proj_bias,
    ln2_gain,
    ln2_bias,
    fc1_weight,
    fc1_bias,
    fc2_weight,
    fc2_bias,
    out_grad,
):
    image_count, slot_count, width = images.shape
    heads = frequencies.shape[1]
    head_size = 2 * frequencies.shape[2]
    row_count = image_count * slot_count
    score_scale = 1.0 / math.sqrt(head_size)
    kept = keep_mask.astype(jnp.float32)
    kept_col = kept.reshape(row_count, 1)
    place = jnp.arange(slot_count)
    across = (place // GRID).astype(jnp.float32)
    downward = (place % GRID).astype(jnp.float32)
    angle = (
        across[:, None, None] * frequencies[0][None]
        + downward[:, None, None] * frequencies[1][None]
    )
    cosine = jnp.cos(angle)
    sine = jnp.sin(angle)

    def masked_scores(queries, key_rows, kept_row):
        scores = (
            jnp.einsum("qhd,khd->hqk", queries, key_rows, preferred_element_type=jnp.float32)
            * score_scale
        )
        return jnp.where(kept_row[None, None, :] > 0, scores, MASKED_SCORE)

    def attend_image(block_item):
        queries, key_rows, values, kept_row = block_item
        scores = masked_scores(queries, key_rows, kept_row)
        row_max = jnp.max(scores, axis=-1, keepdims=True)
        weights = jnp.exp(scores - row_max)
        row_total = jnp.sum(weights, axis=-1, keepdims=True)
        low_weights = (weights / row_total).astype(jnp.bfloat16)
        mixed = jnp.einsum("hqk,khd->qhd", low_weights, values, preferred_element_type=jnp.float32)
        return (mixed, (row_max + jnp.log(row_total))[..., 0])

    def attend_back(block_item):
        queries, key_rows, values, grad_mixed, log_total, kept_row = block_item
        scores = masked_scores(queries, key_rows, kept_row)
        weights = jnp.exp(scores - log_total[..., None])
        low_weights = weights.astype(jnp.bfloat16)
        grad_weights = jnp.einsum(
            "qhd,khd->hqk", grad_mixed, values, preferred_element_type=jnp.float32
        )
        inner = jnp.sum(weights * grad_weights, axis=-1, keepdims=True)
        grad_scores = (weights * (grad_weights - inner)).astype(jnp.bfloat16)
        grad_query = (
            jnp.einsum("hqk,khd->qhd", grad_scores, key_rows, preferred_element_type=jnp.float32)
            * score_scale
        )
        grad_keys = (
            jnp.einsum("hqk,qhd->khd", grad_scores, queries, preferred_element_type=jnp.float32)
            * score_scale
        )
        grad_values = jnp.einsum(
            "hqk,qhd->khd", low_weights, grad_mixed, preferred_element_type=jnp.float32
        )
        return (grad_query, grad_keys, grad_values)

    inputs = images.astype(jnp.float32).reshape(row_count, width)
    unit_one, inverse_one = normalize(inputs)
    normed_one = (unit_one * ln1_gain + ln1_bias).astype(jnp.bfloat16)
    packed = jnp.dot(normed_one, qkv_weight, preferred_element_type=jnp.float32) + qkv_bias
    packed = packed.reshape(image_count, slot_count, 3, heads, head_size)
    turned_query = rotate(packed[:, :, 0], cosine, sine)
    turned_keys = rotate(packed[:, :, 1], cosine, sine)
    low_query = turned_query.astype(jnp.bfloat16)
    low_keys = turned_keys.astype(jnp.bfloat16)
    low_values = packed[:, :, 2].astype(jnp.bfloat16)
    mixed, log_totals = lax.map(attend_image, (low_query, low_keys, low_values, kept))
    low_mixed = mixed.reshape(row_count, width).astype(jnp.bfloat16)
    resid = inputs + jnp.dot(low_mixed, proj_weight, preferred_element_type=jnp.float32) + proj_bias
    unit_two, inverse_two = normalize(resid)
    normed_two = (unit_two * ln2_gain + ln2_bias).astype(jnp.bfloat16)
    grad_rows = kept_col * out_grad.astype(jnp.float32).reshape(row_count, width)
    low_grad_rows = grad_rows.astype(jnp.bfloat16)
    all_normed = lax.all_gather(normed_two, "tensor", axis=0, tiled=True)
    hidden = jnp.dot(all_normed, fc1_weight, preferred_element_type=jnp.float32) + fc1_bias.astype(
        jnp.float32
    )
    low_active = gelu_exact(hidden).astype(jnp.bfloat16)
    piece = low_active
    mlp_out = lax.psum_scatter(
        jnp.dot(piece, fc2_weight, preferred_element_type=jnp.float32).astype(jnp.bfloat16),
        "tensor",
        scatter_dimension=0,
        tiled=True,
    ).astype(jnp.float32)
    all_grads = lax.all_gather(low_grad_rows, "tensor", axis=0, tiled=True)
    fc2_weight_grad = contract_rows(low_active, all_grads)
    grad_active = contract_cols(all_grads, fc2_weight)
    low_grad_hidden = (grad_active * gelu_slope(hidden)).astype(jnp.bfloat16)
    fc1_weight_grad = contract_rows(all_normed, low_grad_hidden)
    fc1_bias_grad = jnp.sum(low_grad_hidden.astype(jnp.float32), axis=0)
    piece = low_grad_hidden
    grad_normed_two = lax.psum_scatter(
        contract_cols(piece, fc1_weight).astype(jnp.bfloat16),
        "tensor",
        scatter_dimension=0,
        tiled=True,
    ).astype(jnp.float32)
    block_out = (kept_col * (resid + mlp_out + fc2_bias)).astype(jnp.bfloat16).reshape(images.shape)
    fc2_bias_grad = jnp.sum(grad_rows, axis=0)
    ln2_gain_grad = jnp.sum(grad_normed_two * unit_two, axis=0)
    ln2_bias_grad = jnp.sum(grad_normed_two, axis=0)
    grad_resid = grad_rows + norm_back(grad_normed_two * ln2_gain, unit_two, inverse_two)
    low_grad_branch = grad_resid.astype(jnp.bfloat16)
    proj_bias_grad = jnp.sum(low_grad_branch.astype(jnp.float32), axis=0)
    proj_weight_grad = contract_rows(low_mixed, low_grad_branch)
    low_grad_mixed = contract_cols(low_grad_branch, proj_weight).astype(jnp.bfloat16)
    low_grad_mixed = low_grad_mixed.reshape(image_count, slot_count, heads, head_size)
    grad_query, grad_keys, grad_values = lax.map(
        attend_back, (low_query, low_keys, low_values, low_grad_mixed, log_totals, kept)
    )
    angle_grad = angle_part(grad_query, turned_query) + angle_part(grad_keys, turned_keys)
    freq_grad = jnp.stack(
        [
            jnp.einsum("nshj,s->hj", angle_grad, across),
            jnp.einsum("nshj,s->hj", angle_grad, downward),
        ]
    )
    grad_packed = jnp.stack(
        [rotate_back(grad_query, cosine, sine), rotate_back(grad_keys, cosine, sine), grad_values],
        axis=2,
    ).reshape(row_count, 3 * width)
    low_grad_packed = grad_packed.astype(jnp.bfloat16)
    qkv_bias_grad = jnp.sum(low_grad_packed.astype(jnp.float32), axis=0)
    qkv_weight_grad = contract_rows(normed_one, low_grad_packed)
    grad_normed_one = contract_cols(low_grad_packed, qkv_weight)
    ln1_gain_grad = jnp.sum(grad_normed_one * unit_one, axis=0)
    ln1_bias_grad = jnp.sum(grad_normed_one, axis=0)
    input_grad = grad_resid + norm_back(grad_normed_one * ln1_gain, unit_one, inverse_one)
    input_grad = input_grad.astype(jnp.bfloat16).reshape(images.shape)
    (
        ln1_gain_grad,
        ln1_bias_grad,
        qkv_weight_grad,
        qkv_bias_grad,
        freq_grad,
        proj_weight_grad,
        proj_bias_grad,
        ln2_gain_grad,
        ln2_bias_grad,
        fc2_bias_grad,
    ) = lax.psum(
        (
            ln1_gain_grad,
            ln1_bias_grad,
            qkv_weight_grad,
            qkv_bias_grad,
            freq_grad,
            proj_weight_grad,
            proj_bias_grad,
            ln2_gain_grad,
            ln2_bias_grad,
            fc2_bias_grad,
        ),
        ("dp", "tensor"),
    )
    fc1_weight_grad, fc1_bias_grad, fc2_weight_grad = (
        lax.psum(fc1_weight_grad.astype(jnp.bfloat16), "dp").astype(jnp.float32),
        lax.psum(fc1_bias_grad.astype(jnp.bfloat16), "dp").astype(jnp.float32),
        lax.psum(fc2_weight_grad.astype(jnp.bfloat16), "dp").astype(jnp.float32),
    )
    freq_norm = jnp.sqrt(jnp.sum(freq_grad * freq_grad))
    local_square = jnp.float32(0.0)
    for member in (
        ln1_gain_grad,
        ln1_bias_grad,
        qkv_weight_grad,
        qkv_bias_grad,
        proj_weight_grad,
        proj_bias_grad,
        ln2_gain_grad,
        ln2_bias_grad,
        fc2_bias_grad,
    ):
        local_square = local_square + jnp.sum(member * member)
    rest_norm = jnp.sqrt(local_square)
    return (
        block_out,
        input_grad,
        ln1_gain_grad,
        ln1_bias_grad,
        qkv_weight_grad,
        qkv_bias_grad,
        freq_grad,
        proj_weight_grad,
        proj_bias_grad,
        ln2_gain_grad,
        ln2_bias_grad,
        fc1_weight_grad,
        fc1_bias_grad,
        fc2_weight_grad,
        fc2_bias_grad,
        freq_norm,
        rest_norm,
    )


def solution(mesh):
    placed = (
        P(("dp", "tensor"), None, None),
        P(("dp", "tensor"), None),
        P(),
        P(),
        P(),
        P(),
        P(),
        P(),
        P(),
        P(),
        P(),
        P(None, "tensor"),
        P("tensor"),
        P("tensor", None),
        P(),
        P(("dp", "tensor"), None, None),
    )
    return jax.shard_map(
        body,
        mesh=mesh,
        in_specs=placed,
        out_specs=(
            P(("dp", "tensor"), None, None),
            P(("dp", "tensor"), None, None),
            P(),
            P(),
            P(),
            P(),
            P(),
            P(),
            P(),
            P(),
            P(),
            P(None, "tensor"),
            P("tensor"),
            P("tensor", None),
            P(),
            P(),
            P(),
        ),
        check_vma=False,
    )
```

profile of v0, /device:TPU:0, one launch (start us, length us, event | category | flops | bytes accessed | tf_op | source)
XLA Modules:
  0.0 956.7 jit_solution(10277349435607257077)
XLA Ops:
  9.2 2.7 multiply_reduce_fusion.6
  19.0 6.8 convolution_add_fusion
  25.8 12.7 %copy.89 = f32[1152,2304]{0,1:T(8,128)} copy(f32[1152,2304]{1,0:T(8,128)} %convolution_add_fusion) | data formatting | bytes 21233664 | tf_op jit(solution)/shard_map/add | solution.py:161
  38.5 15.3 %reshape.232 = f32[2,576,3,12,64]{1,0,4,3,2:T(2,128)} reshape(f32[1152,2304]{0,1:T(8,128)} %copy.89) | data formatting | bytes 21233664 | tf_op jit(solution)/shard_map/reshape | solution.py:162
  53.8 4.8 fusion.60
  58.6 10.8 %fusion.80 = (f32[2,576,1,12,64]{1,0,4,3,2:T(2,128)}, f32[2,576,1,12,64]{1,0,4,3,2:T(2,128)}) fusion(f32[2,576,3,12,64]{1,0,4,3,2:T(2,128)} %reshape.232), kind=kLoop, calls=%fused_computation.163 | loop fusion | bytes 14155776 | tf_op jit(solution)/shard_map/slice | solution.py:164
  70.7 3.1 copy.123
  73.8 3.6 copy.94
  78.8 3.6 fusion.61
  86.9 71.6 %while.28 = (s32[]{:T(128)}, bf16[2,576,12,64]{1,3,2,0:T(8,128)(2,1)}, f32[2,12,576]{2,1,0:T(8,128)}, bf16[2,576,12,64]{1,3,2,0:T(8,128)(2,1)}, f32[2,576]{1,0:T...) while((s32[]{:T(128)}, bf16[2,576,12,64]{1,3,2,0:T(8,128)(2,1)}, ...), condition=%wide.region_5.6_spmd.clone, body=%wide.region_2.5_spmd.sunk.clone | while | flops 1066985280 | bytes 55221964 | solution.py:168
  88.1 11.9 %fusion.141 = (f32[12,576]{1,0:T(8,128)}, f32[12,576,576]{1,2,0:T(8,128)}) fusion(pred[576]{0:T(1024)(128)(4,1)S(1)} %compare_reduce_fusion.6, bf16[2,576,12,64]{1,3,2,0:T(8,128)(2,1)} %get-tuple-element.496, s32[]{:T(128)S(6)} %copy.125, bf16[2,576,12,64]{1,3,2,0:T(8,128)(2,1)} %get-tuple-element.495), kind=kOutput, calls=%fused_computation.3.clone.1.clone | convolution fusion | flops 521544960 | bytes 17920576 | tf_op jit(solution)/shard_map/while/body/eval_jaxpr/qhd,khd->hqk/dot_general | solution.py:120
  100.0 10.3 %fusion.142 = f32[12,576]{1,0:T(8,128)} fusion(f32[12,576,576]{1,2,0:T(8,128)} %get-tuple-element.442, f32[12,576]{1,0:T(8,128)} %get-tuple-element.443, pred[576]{0:T(1024)(128)(4,1)S(1)} %compare_reduce_fusion.6), kind=kLoop, calls=%fused_computation.4.clone.1.clone | loop fusion | flops 15918336 | bytes 15981120 | tf_op jit(solution)/shard_map/while/body/eval_jaxpr/reduce_sum | solution.py:130
  110.4 11.8 %bitcast_dynamic-update-slice_fusion.15 = bf16[2,576,12,64]{1,3,2,0:T(8,128)(2,1)} fusion(bf16[2,576,12,64]{1,3,2,0:T(8,128)(2,1)} %get-tuple-element.484, s32[]{:T(128)S(6)} %copy.125, f32[12,576,576]{1,2,0:T(8,128)} %get-tuple-element.442, f32[12,576]{1,0:T(8,128)} %fusion.142, f32[12,576]{1,0:T(8,128)} %get-tuple-element.443, ...), kind=kOutput, calls=%fused_computation.6.clone.1.clone | convolution fusion | flops 529514496 | bytes 20530752 | tf_op jit(solution)/shard_map/while/body/eval_jaxpr/hqk,khd->qhd/dot_general | solution.py:132
  123.5 12.0 %fusion.141 = (f32[12,576]{1,0:T(8,128)}, f32[12,576,576]{1,2,0:T(8,128)}) fusion(pred[576]{0:T(1024)(128)(4,1)S(1)} %compare_reduce_fusion.6, bf16[2,576,12,64]{1,3,2,0:T(8,128)(2,1)} %get-tuple-element.496, s32[]{:T(128)S(6)} %copy.125, bf16[2,576,12,64]{1,3,2,0:T(8,128)(2,1)} %get-tuple-element.495), kind=kOutput, calls=%fused_computation.3.clone.1.clone | convolution fusion | flops 521544960 | bytes 17920576 | tf_op jit(solution)/shard_map/while/body/eval_jaxpr/qhd,khd->hqk/dot_general | solution.py:120
  135.5 10.3 %fusion.142 = f32[12,576]{1,0:T(8,128)} fusion(f32[12,576,576]{1,2,0:T(8,128)} %get-tuple-element.442, f32[12,576]{1,0:T(8,128)} %get-tuple-element.443, pred[576]{0:T(1024)(128)(4,1)S(1)} %compare_reduce_fusion.6), kind=kLoop, calls=%fused_computation.4.clone.1.clone | loop fusion | flops 15918336 | bytes 15981120 | tf_op jit(solution)/shard_map/while/body/eval_jaxpr/reduce_sum | solution.py:130
  145.8 11.8 %bitcast_dynamic-update-slice_fusion.15 = bf16[2,576,12,64]{1,3,2,0:T(8,128)(2,1)} fusion(bf16[2,576,12,64]{1,3,2,0:T(8,128)(2,1)} %get-tuple-element.484, s32[]{:T(128)S(6)} %copy.125, f32[12,576,576]{1,2,0:T(8,128)} %get-tuple-element.442, f32[12,576]{1,0:T(8,128)} %fusion.142, f32[12,576]{1,0:T(8,128)} %get-tuple-element.443, ...), kind=kOutput, calls=%fused_computation.6.clone.1.clone | convolution fusion | flops 529514496 | bytes 20530752 | tf_op jit(solution)/shard_map/while/body/eval_jaxpr/hqk,khd->qhd/dot_general | solution.py:132
  158.5 4.8 copy.95
  163.3 5.0 convert_element_type.140
  168.3 4.2 fusion.83
  177.7 3.0 fusion.59
  182.1 47.9 %all-gather.3.cloned.1.call-done = bf16[4608,768]{1,0:T(8,128)(2,1)} async-done(((bf16[1152,768]{1,0:T(8,128)(2,1)}), bf16[4608,768]{1,0:T(8,128)(2,1)}) %all-gather.3.cloned.1.call-update) | async-done | bytes 7077904 | tf_op jit(solution)/shard_map/all_gather | solution.py:175
  230.0 14.3 %multiply_convert_fusion.1 = (bf16[4608,768]{1,0:T(8,128)(2,1)}, f32[4608,768]{1,0:T(8,128)}) fusion(f32[768]{0:T(1024)} %convert_element_type.142, bf16[4608,768]{1,0:T(8,128)(2,1)} %all-gather.3.cloned.1.call-done, bf16[768,768]{1,0:T(8,128)(2,1)} %param.31), kind=kOutput, calls=%fused_computation.61 | convolution fusion | flops 5457051648 | bytes 29494272 | tf_op jit(solution)/shard_map/dot_general | solution.py:176
  244.2 38.8 %all-gather.5.cloned.1.call-done = bf16[4608,768]{1,0:T(8,128)(2,1)} async-done(((bf16[1152,768]{1,0:T(8,128)(2,1)}), bf16[4608,768]{1,0:T(8,128)(2,1)}) %all-gather.5.cloned.1.call-update) | async-done | bytes 7077904 | tf_op jit(solution)/shard_map/all_gather | solution.py:187
  283.0 11.8 %convolution_convert_fusion.3 = bf16[768,768]{1,0:T(8,128)(2,1)} fusion(bf16[4608,768]{1,0:T(8,128)(2,1)} %get-tuple-element.311, bf16[4608,768]{1,0:T(8,128)(2,1)} %all-gather.5.cloned.1.call-done), kind=kOutput, calls=%fused_computation.119 | convolution fusion | flops 5436407808 | bytes 15335424 | tf_op jit(solution)/shard_map/dot_general | solution.py:72
  294.8 13.2 %fusion.84 = (bf16[768]{0:T(1024)(128)(2,1)}, bf16[4608,768]{1,0:T(8,128)(2,1)S(1)}) fusion(f32[4608,768]{1,0:T(8,128)} %get-tuple-element.312, f32[768]{0:T(1024)S(1)} %copy-done.37, bf16[4608,768]{1,0:T(8,128)(2,1)S(1)} %copy-done.39, bf16[768,768]{1,0:T(8,128)(2,1)S(1)} %copy-done.40), kind=kOutput, calls=%fused_computation.167 | convolution fusion | flops 5478284288 | bytes 29495808 | tf_op jit(solution)/shard_map/dot_general | solution.py:78
  307.9 2.9 copy-done.44
  310.9 7.1 convolution_convert_fusion.4
  318.0 10.5 %convolution_convert_fusion = bf16[4608,768]{1,0:T(8,128)(2,1)} fusion(bf16[4608,768]{1,0:T(8,128)(2,1)} %copy-done.44, bf16[768,768]{1,0:T(8,128)(2,1)} %param.31), kind=kOutput, calls=%fused_computation.66 | convolution fusion | flops 5439356928 | bytes 15335424 | tf_op jit(solution)/shard_map/dot_general | solution.py:78
  328.6 10.1 %convolution_convert_fusion.1 = bf16[4608,768]{1,0:T(8,128)(2,1)} fusion(bf16[4608,768]{1,0:T(8,128)(2,1)} %get-tuple-element.311, bf16[768,768]{1,0:T(8,128)(2,1)} %param.33), kind=kOutput, calls=%fused_computation.67 | convolution fusion | flops 5439356928 | bytes 15335424 | tf_op jit(solution)/shard_map/dot_general | solution.py:182
  343.8 3.5 add_convert_fusion
  347.3 22.1 %psum.101 = bf16[768]{0:T(1024)(128)(2,1)} all-reduce(bf16[768]{0:T(1024)(128)(2,1)} %get-tuple-element.314), channel_id=1, replica_groups=mesh['dp'=8,'tensor'=4] {'dp'}, use_global_device_ids=true, to_apply=%region_35.36 | all-reduce | flops 768 | bytes 3072 | tf_op jit(solution)/shard_map/psum | solution.py:260
  370.7 56.7 %all-reduce.8.cloned.1.call-done = (bf16[768,768]{1,0:T(8,128)(2,1)}, bf16[768,768]{1,0:T(8,128)(2,1)}) async-done(((bf16[768,768]{1,0:T(8,128)(2,1)}, bf16[768,768]{1,0:T(8,128)(2,1)}), (bf16[768,768]{1,0:T(8,128)(2,1)}, bf16[768,768]{1,0:T(8,128)(2,1)})) %all-reduce.8.cloned.1.call-update) | async-done | bytes 2359312 | tf_op jit(solution)/shard_map/psum | solution.py:259
  427.4 2.9 convert_element_type.162
  432.0 60.7 %reduce-scatter.5.cloned.1.call-done = bf16[1152,768]{1,0:T(8,128)(2,1)} async-done(((bf16[4608,768]{1,0:T(8,128)(2,1)}), bf16[1152,768]{1,0:T(8,128)(2,1)}) %reduce-scatter.5.cloned.1.call-update) | async-done | bytes 1769488 | tf_op jit(solution)/shard_map/reduce_scatter | solution.py:194
  492.7 4.7 fusion.57
  498.6 60.3 %reduce-scatter.3.cloned.1.call-done = bf16[1152,768]{1,0:T(8,128)(2,1)} async-done(((bf16[4608,768]{1,0:T(8,128)(2,1)}), bf16[1152,768]{1,0:T(8,128)(2,1)}) %reduce-scatter.3.cloned.1.call-update) | async-done | bytes 1769488 | tf_op jit(solution)/shard_map/reduce_scatter | solution.py:181
  558.8 6.3 convert_reduce_fusion.2
  565.1 3.1 fusion.72
  568.3 2.8 convolution_convert_fusion.2
  571.1 3.9 copy.96
  574.9 5.4 reshape.235
  580.3 3.2 copy.97
  583.6 112.7 %while.29 = (s32[]{:T(128)}, f32[2,576,12,64]{1,3,2,0:T(8,128)}, f32[2,576,12,64]{1,3,2,0:T(8,128)}, bf16[2,576,12,64]{1,3,2,0:T(8,128)(2,1)}, bf16[2,576,12,64]...) while((s32[]{:T(128)}, f32[2,576,12,64]{1,3,2,0:T(8,128)}, ...), condition=%wide.region_14.15_spmd.clone, body=%wide.region_12.14_spmd.sunk.clone | while | flops 2608637696 | bytes 233113376 | solution.py:210
  585.2 10.2 %fusion.151 = f32[12,576,576]{1,2,0:T(8,128)} fusion(bf16[2,576,12,64]{1,3,2,0:T(8,128)(2,1)} %get-tuple-element.523, s32[]{:T(128)S(6)} %copy.135, bf16[2,576,12,64]{1,3,2,0:T(8,128)(2,1)} %get-tuple-element.521), kind=kOutput, calls=%fused_computation.34.clone.1.clone | convolution fusion | flops 509607936 | bytes 17892352 | tf_op jit(solution)/shard_map/while/body/eval_jaxpr/qhd,khd->hqk/dot_general | solution.py:120
  595.4 10.4 %bitcast_dynamic-update-slice_fusion.19 = bf16[2,576,12,64]{1,3,2,0:T(8,128)(2,1)S(1)} fusion(bf16[2,576,12,64]{1,3,2,0:T(8,128)(2,1)S(1)} %copy-done.8, s32[]{:T(128)S(6)} %copy.135, f32[12,576,576]{1,2,0:T(8,128)} %fusion.151, f32[12,576]{1,0:T(8,128)S(1)} %dynamic-slice_bitcast_fusion.3, pred[576]{0:T(1024)(128)(4,1)S(1)} %compare_reduce_fusion.7, ...), kind=kOutput, calls=%fused_computation.26.clone.1.clone | convolution fusion | flops 525533184 | bytes 18720768 | tf_op jit(solution)/shard_map/while/body/eval_jaxpr/hqk,qhd->khd/dot_general | solution.py:153
  605.9 13.3 %multiply_reduce_fusion.19 = (f32[12,576]{1,0:T(8,128)S(1)}, f32[12,576,576]{1,2,0:T(8,128)}) fusion(f32[12,576,576]{1,2,0:T(8,128)} %fusion.151, f32[12,576]{1,0:T(8,128)S(1)} %dynamic-slice_bitcast_fusion.3, pred[576]{0:T(1024)(128)(4,1)S(1)} %compare_reduce_fusion.7, bf16[2,576,12,64]{1,3,2,0:T(8,128)(2,1)S(1)} %copy-done.6, ...), kind=kOutput, calls=%fused_computation.21.clone.1.clone | convolution fusion | flops 529507584 | bytes 33887232 | tf_op jit(solution)/shard_map/while/body/eval_jaxpr/qhd,khd->hqk/dot_general | solution.py:140
  619.2 14.1 %multiply_convert_fusion.5 = bf16[12,576,576]{1,2,0:T(8,128)(2,1)S(1)} fusion(f32[12,576,576]{1,2,0:T(8,128)} %get-tuple-element.463, f32[12,576,576]{1,2,0:T(8,128)} %fusion.151, f32[12,576]{1,0:T(8,128)S(1)} %get-tuple-element.464, f32[12,576]{1,0:T(8,128)S(1)} %dynamic-slice_bitcast_fusion.3, pred[576]{0:T(1024)(128)(4,1)S(1)} %compare_reduce_fusion.7), kind=kLoop, calls=%fused_computation.20.clone.1.clone | loop fusion | flops 23887872 | bytes 39868992 | tf_op jit(solution)/shard_map/while/body/eval_jaxpr/convert_element_type | solution.py:144
  633.3 2.7 bitcast_dynamic-update-slice_fusion.18
  641.4 10.2 %fusion.151 = f32[12,576,576]{1,2,0:T(8,128)} fusion(bf16[2,576,12,64]{1,3,2,0:T(8,128)(2,1)} %get-tuple-element.523, s32[]{:T(128)S(6)} %copy.135, bf16[2,576,12,64]{1,3,2,0:T(8,128)(2,1)} %get-tuple-element.521), kind=kOutput, calls=%fused_computation.34.clone.1.clone | convolution fusion | flops 509607936 | bytes 17892352 | tf_op jit(solution)/shard_map/while/body/eval_jaxpr/qhd,khd->hqk/dot_general | solution.py:120
  651.6 10.4 %bitcast_dynamic-update-slice_fusion.19 = bf16[2,576,12,64]{1,3,2,0:T(8,128)(2,1)S(1)} fusion(bf16[2,576,12,64]{1,3,2,0:T(8,128)(2,1)S(1)} %copy-done.8, s32[]{:T(128)S(6)} %copy.135, f32[12,576,576]{1,2,0:T(8,128)} %fusion.151, f32[12,576]{1,0:T(8,128)S(1)} %dynamic-slice_bitcast_fusion.3, pred[576]{0:T(1024)(128)(4,1)S(1)} %compare_reduce_fusion.7, ...), kind=kOutput, calls=%fused_computation.26.clone.1.clone | convolution fusion | flops 525533184 | bytes 18720768 | tf_op jit(solution)/shard_map/while/body/eval_jaxpr/hqk,qhd->khd/dot_general | solution.py:153
  662.1 13.3 %multiply_reduce_fusion.19 = (f32[12,576]{1,0:T(8,128)S(1)}, f32[12,576,576]{1,2,0:T(8,128)}) fusion(f32[12,576,576]{1,2,0:T(8,128)} %fusion.151, f32[12,576]{1,0:T(8,128)S(1)} %dynamic-slice_bitcast_fusion.3, pred[576]{0:T(1024)(128)(4,1)S(1)} %compare_reduce_fusion.7, bf16[2,576,12,64]{1,3,2,0:T(8,128)(2,1)S(1)} %copy-done.6, ...), kind=kOutput, calls=%fused_computation.21.clone.1.clone | convolution fusion | flops 529507584 | bytes 33887232 | tf_op jit(solution)/shard_map/while/body/eval_jaxpr/qhd,khd->hqk/dot_general | solution.py:140
  675.4 14.1 %multiply_convert_fusion.5 = bf16[12,576,576]{1,2,0:T(8,128)(2,1)S(1)} fusion(f32[12,576,576]{1,2,0:T(8,128)} %get-tuple-element.463, f32[12,576,576]{1,2,0:T(8,128)} %fusion.151, f32[12,576]{1,0:T(8,128)S(1)} %get-tuple-element.464, f32[12,576]{1,0:T(8,128)S(1)} %dynamic-slice_bitcast_fusion.3, pred[576]{0:T(1024)(128)(4,1)S(1)} %compare_reduce_fusion.7), kind=kLoop, calls=%fused_computation.20.clone.1.clone | loop fusion | flops 23887872 | bytes 39868992 | tf_op jit(solution)/shard_map/while/body/eval_jaxpr/convert_element_type | solution.py:144
  696.3 5.2 multiply_add_fusion.1
  704.9 5.6 copy.99
  710.6 12.3 %convert_element_type.155 = bf16[1152,2304]{0,1:T(8,128)(2,1)} reshape(bf16[2,576,3,12,64]{1,0,4,3,2:T(2,128)(2,1)} %copy.99) | data formatting | bytes 10616832 | tf_op jit(solution)/shard_map/convert_element_type | solution.py:224
  722.9 10.8 %fusion.85 = f32[768,2304]{1,0:T(8,128)} fusion(bf16[1152,768]{1,0:T(8,128)(2,1)} %bitcast.188, bf16[1152,2304]{0,1:T(8,128)(2,1)} %convert_element_type.155), kind=kOutput, calls=%fused_computation.168 | convolution fusion | flops 4076863488 | bytes 14155776 | tf_op jit(solution)/shard_map/dot_general | solution.py:72
  733.7 8.2 add_reduce_fusion
  746.9 11.0 %multiply_reduce_fusion.3 = (f32[768]{0:T(1024)}, f32[1152]{0:T(1024)}, f32[1152]{0:T(1024)}, f32[768]{0:T(1024)}, f32[1152,768]{1,0:T(8,128)}) fusion(bf16[2,576,768]{2,1,0:T(8,128)(2,1)} %param.20, f32[1152]{0:T(1024)S(1)} %copy-done.30, f32[1152]{0:T(1024)S(1)} %copy-done.29, f32[768]{0:T(1024)} %param.22, bf16[1152,2304]{0,1:T(8,128)(2,1)} %convert_element_type.155, ...), kind=kOutput, calls=%fused_computation.93 | convolution fusion | flops 4085707008 | bytes 14183424 | tf_op jit(solution)/shard_map/dot_general | solution.py:78
  757.8 41.8 %all-reduce = (f32[768]{0:T(1024)}, f32[768]{0:T(1024)}, f32[2304]{0:T(1024)}, f32[2,12,32]{2,1,0:T(8,128)}, f32[768]{0:T(1024)}, /*index=5*/f32[768]{0:T(1024)}, f32[768]{0:T(1024)}, f32[768]{0:T(1024)}) all-reduce(f32[768]{0:T(1024)} %get-tuple-element.228, ...), channel_id=1, replica_groups=mesh['dp'=8,'tensor'=4] {'dp','tensor'}, use_global_device_ids=true, to_apply=%region_18.19 | all-reduce | flops 7680 | bytes 61440 | tf_op jit(solution)/shard_map/psum | solution.py:243
  815.0 5.4 add_convert_fusion.1
  820.3 106.0 %all-reduce.6.cloned.1.call-done = (f32[768,2304]{1,0:T(8,128)}, f32[768,768]{1,0:T(8,128)}) async-done(((f32[768,2304]{1,0:T(8,128)}, f32[768,768]{1,0:T(8,128)}), (f32[768,2304]{1,0:T(8,128)}, f32[768,768]{1,0:T(8,128)})) %all-reduce.6.cloned.1.call-update) | async-done | bytes 9437200 | tf_op jit(solution)/shard_map/psum | solution.py:243
  926.3 2.9 multiply_reduce_fusion.8
  929.2 5.4 multiply_reduce_fusion.1
  939.2 6.6 copy.149
  (197 shorter events, 71.2 us)
Async XLA Ops:
  7.2 11.8 %copy-start = (bf16[768,2304]{1,0:T(8,128)(2,1)S(1)}, bf16[768,2304]{1,0:T(8,128)(2,1)}, u32[]{:S(2)}) copy-start(bf16[768,2304]{1,0:T(8,128)(2,1)} %param.24) | copy-start | bytes 10616836
  7.2 222.8 %all-gather.3.cloned.1.call-start = ((), (), s32[]{:S(2)}) async-start(), calls=%async_computation.2 | async-start | bytes 8847360 | tf_op jit(solution)/shard_map/all_gather | solution.py:175
  9.2 9.8 %copy-start.27 = (f32[2,576]{1,0:T(2,128)}, f32[2,576]{1,0:T(2,128)S(1)}, u32[]{:S(2)}) copy-start(f32[2,576]{1,0:T(2,128)S(1)} %broadcast_multiply_fusion.5) | copy-start | bytes 13828
  12.0 13.8 %copy-start.28 = (f32[1152]{0:T(1024)}, f32[1152]{0:T(1024)S(1)}, u32[]{:S(2)}) copy-start(f32[1152]{0:T(1024)S(1)} %div.47) | copy-start | bytes 13828
  16.8 2.2 copy-start.42
  58.6 12.1 %copy-start.34 = (f32[2,12,32]{2,0,1:T(2,128)S(1)}, f32[2,12,32]{2,0,1:T(2,128)}, u32[]{:S(2)}) copy-start(f32[2,12,32]{2,0,1:T(2,128)} %param.26) | copy-start | bytes 9220
  70.7 6.8 copy-start.15
  70.7 6.8 copy-start.16
  77.5 1.3 copy-start.31
  78.7 5.0 copy-start.4
  78.7 5.0 copy-start.5
  82.3 1.4 copy-start.17
  82.3 1.4 copy-start.18
  110.3 11.8 %copy-start.21 = (f32[12,576]{1,0:T(8,128)S(1)}, f32[12,576]{1,0:T(8,128)}, u32[]{:S(2)}) copy-start(f32[12,576]{1,0:T(8,128)} %get-tuple-element.443) | copy-start | bytes 82948 | tf_op jit(solution)/shard_map/while
  110.4 11.8 %copy-start.22 = (f32[12,576]{1,0:T(8,128)S(1)}, f32[12,576]{1,0:T(8,128)}, u32[]{:S(2)}) copy-start(f32[12,576]{1,0:T(8,128)} %fusion.142) | copy-start | bytes 82948 | tf_op jit(solution)/shard_map/while
  110.4 11.8 %copy-start.25 = (f32[2,12,576]{2,1,0:T(8,128)S(1)}, f32[2,12,576]{2,1,0:T(8,128)}, u32[]{:S(2)}) copy-start(f32[2,12,576]{2,1,0:T(8,128)} %get-tuple-element.485) | copy-start | bytes 165892 | tf_op jit(solution)/shard_map/while
  145.8 11.8 %copy-start.21 = (f32[12,576]{1,0:T(8,128)S(1)}, f32[12,576]{1,0:T(8,128)}, u32[]{:S(2)}) copy-start(f32[12,576]{1,0:T(8,128)} %get-tuple-element.443) | copy-start | bytes 82948 | tf_op jit(solution)/shard_map/while
  145.8 11.8 %copy-start.22 = (f32[12,576]{1,0:T(8,128)S(1)}, f32[12,576]{1,0:T(8,128)}, u32[]{:S(2)}) copy-start(f32[12,576]{1,0:T(8,128)} %fusion.142) | copy-start | bytes 82948 | tf_op jit(solution)/shard_map/while
  145.8 11.8 %copy-start.25 = (f32[2,12,576]{2,1,0:T(8,128)S(1)}, f32[2,12,576]{2,1,0:T(8,128)}, u32[]{:S(2)}) copy-start(f32[2,12,576]{2,1,0:T(8,128)} %get-tuple-element.485) | copy-start | bytes 165892 | tf_op jit(solution)/shard_map/while
  158.5 9.8 %copy-start.43 = (f32[768]{0:T(1024)S(1)}, f32[768]{0:T(1024)}, u32[]{:S(2)}) copy-start(f32[768]{0:T(1024)} %param.28) | copy-start | bytes 9220
  172.5 1.9 copy-start.3
  172.5 1.9 copy-start.33
  172.5 1.9 copy-start.38
  176.3 106.7 %all-gather.5.cloned.1.call-start = ((), (), s32[]{:S(2)}) async-start(), calls=%async_computation.4 | async-start | bytes 8847360 | tf_op jit(solution)/shard_map/all_gather | solution.py:187
  180.7 246.7 %all-reduce.8.cloned.1.call-start = ((), (), s32[]{:S(2)}) async-start(), calls=%async_computation.7 | async-start | bytes 4718592 | tf_op jit(solution)/shard_map/psum | solution.py:259
  283.0 11.8 %copy-start.37 = (f32[768]{0:T(1024)S(1)}, f32[768]{0:T(1024)}, u32[]{:S(2)}) copy-start(f32[768]{0:T(1024)} %convert_element_type.142) | copy-start | bytes 9220
  283.0 11.8 %copy-start.39 = (bf16[4608,768]{1,0:T(8,128)(2,1)S(1)}, bf16[4608,768]{1,0:T(8,128)(2,1)}, u32[]{:S(2)}) copy-start(bf16[4608,768]{1,0:T(8,128)(2,1)} %all-gather.5.cloned.1.call-done) | copy-start | bytes 21233668
  283.0 11.8 %copy-start.40 = (bf16[768,768]{1,0:T(8,128)(2,1)S(1)}, bf16[768,768]{1,0:T(8,128)(2,1)}, u32[]{:S(2)}) copy-start(bf16[768,768]{1,0:T(8,128)(2,1)} %param.33) | copy-start | bytes 3538948
  283.0 27.9 %slice-start = ((s8[7077888]{0:T(1024)(128)(4,1)}), s8[4194304]{0:T(1024)(128)(4,1)S(1)}, s32[]{:S(2)}) async-start(s8[7077888]{0:T(1024)(128)(4,1)} %bitcast.190), calls=%async_computation.8 | async-start | bytes 8388608
  294.8 16.1 %slice-start.1 = ((s8[7077888]{0:T(1024)(128)(4,1)}), s8[2883584]{0:T(1024)(128)(4,1)S(1)}, s32[]{:S(2)}) async-start(s8[7077888]{0:T(1024)(128)(4,1)} %bitcast.190), calls=%async_computation.9 | async-start | bytes 5767168
  307.9 2.9 copy-start.44
  318.0 174.7 %reduce-scatter.5.cloned.1.call-start = ((), (), s32[]{:S(2)}) async-start(), calls=%async_computation.5 | async-start | bytes 8847360 | tf_op jit(solution)/shard_map/reduce_scatter | solution.py:194
  328.6 230.3 %reduce-scatter.3.cloned.1.call-start = ((), (), s32[]{:S(2)}) async-start(), calls=%async_computation.3 | async-start | bytes 8847360 | tf_op jit(solution)/shard_map/reduce_scatter | solution.py:181
  338.7 587.6 %all-reduce.6.cloned.1.call-start = ((), (), s32[]{:S(2)}) async-start(), calls=%async_computation.6 | async-start | bytes 18874368 | tf_op jit(solution)/shard_map/psum | solution.py:243
  427.4 2.9 copy-start.24
  558.8 6.3 copy-start.23
  565.1 3.1 copy-start.19
  565.1 3.1 copy-start.41
  585.2 10.2 %copy-start.7 = (bf16[2,576,12,64]{1,3,2,0:T(8,128)(2,1)S(1)}, bf16[2,576,12,64]{1,3,2,0:T(8,128)(2,1)}, u32[]{:S(2)}) copy-start(bf16[2,576,12,64]{1,3,2,0:T(8,128)(2,1)} %get-tuple-element.525) | copy-start | bytes 5308420 | tf_op jit(solution)/shard_map/while
  585.2 10.2 %copy-start.8 = (bf16[2,576,12,64]{1,3,2,0:T(8,128)(2,1)S(1)}, bf16[2,576,12,64]{1,3,2,0:T(8,128)(2,1)}, u32[]{:S(2)}) copy-start(bf16[2,576,12,64]{1,3,2,0:T(8,128)(2,1)} %get-tuple-element.510) | copy-start | bytes 5308420 | tf_op jit(solution)/shard_map/while
  595.4 10.4 %copy-start.6 = (bf16[2,576,12,64]{1,3,2,0:T(8,128)(2,1)S(1)}, bf16[2,576,12,64]{1,3,2,0:T(8,128)(2,1)}, u32[]{:S(2)}) copy-start(bf16[2,576,12,64]{1,3,2,0:T(8,128)(2,1)} %get-tuple-element.526) | copy-start | bytes 5308420 | tf_op jit(solution)/shard_map/while
  605.9 13.3 %copy-start.9 = (bf16[2,576,12,64]{1,3,2,0:T(8,128)(2,1)}, bf16[2,576,12,64]{1,3,2,0:T(8,128)(2,1)S(1)}, u32[]{:S(2)}) copy-start(bf16[2,576,12,64]{1,3,2,0:T(8,128)(2,1)S(1)} %bitcast_dynamic-update-slice_fusion.19) | copy-start | bytes 5308420 | tf_op jit(solution)/shard_map/while
  619.2 14.1 %copy-start.2 = (bf16[2,576,12,64]{1,3,2,0:T(8,128)(2,1)S(1)}, bf16[2,576,12,64]{1,3,2,0:T(8,128)(2,1)}, u32[]{:S(2)}) copy-start(bf16[2,576,12,64]{1,3,2,0:T(8,128)(2,1)} %get-tuple-element.523) | copy-start | bytes 5308420 | tf_op jit(solution)/shard_map/while
  619.2 14.1 %copy-start.11 = (f32[2,576,12,64]{1,3,2,0:T(8,128)S(1)}, f32[2,576,12,64]{1,3,2,0:T(8,128)}, u32[]{:S(2)}) copy-start(f32[2,576,12,64]{1,3,2,0:T(8,128)} %get-tuple-element.509) | copy-start | bytes 10616836 | tf_op jit(solution)/shard_map/while
  633.3 2.7 copy-start.1
  633.3 2.7 copy-start.13
  636.0 1.9 copy-start.12
  637.9 2.0 copy-start.14
  641.4 10.2 %copy-start.7 = (bf16[2,576,12,64]{1,3,2,0:T(8,128)(2,1)S(1)}, bf16[2,576,12,64]{1,3,2,0:T(8,128)(2,1)}, u32[]{:S(2)}) copy-start(bf16[2,576,12,64]{1,3,2,0:T(8,128)(2,1)} %get-tuple-element.525) | copy-start | bytes 5308420 | tf_op jit(solution)/shard_map/while
  641.4 10.2 %copy-start.8 = (bf16[2,576,12,64]{1,3,2,0:T(8,128)(2,1)S(1)}, bf16[2,576,12,64]{1,3,2,0:T(8,128)(2,1)}, u32[]{:S(2)}) copy-start(bf16[2,576,12,64]{1,3,2,0:T(8,128)(2,1)} %get-tuple-element.510) | copy-start | bytes 5308420 | tf_op jit(solution)/shard_map/while
  651.6 10.4 %copy-start.6 = (bf16[2,576,12,64]{1,3,2,0:T(8,128)(2,1)S(1)}, bf16[2,576,12,64]{1,3,2,0:T(8,128)(2,1)}, u32[]{:S(2)}) copy-start(bf16[2,576,12,64]{1,3,2,0:T(8,128)(2,1)} %get-tuple-element.526) | copy-start | bytes 5308420 | tf_op jit(solution)/shard_map/while
  662.0 13.3 %copy-start.9 = (bf16[2,576,12,64]{1,3,2,0:T(8,128)(2,1)}, bf16[2,576,12,64]{1,3,2,0:T(8,128)(2,1)S(1)}, u32[]{:S(2)}) copy-start(bf16[2,576,12,64]{1,3,2,0:T(8,128)(2,1)S(1)} %bitcast_dynamic-update-slice_fusion.19) | copy-start | bytes 5308420 | tf_op jit(solution)/shard_map/while
  675.4 14.1 %copy-start.2 = (bf16[2,576,12,64]{1,3,2,0:T(8,128)(2,1)S(1)}, bf16[2,576,12,64]{1,3,2,0:T(8,128)(2,1)}, u32[]{:S(2)}) copy-start(bf16[2,576,12,64]{1,3,2,0:T(8,128)(2,1)} %get-tuple-element.523) | copy-start | bytes 5308420 | tf_op jit(solution)/shard_map/while
  675.4 14.1 %copy-start.11 = (f32[2,576,12,64]{1,3,2,0:T(8,128)S(1)}, f32[2,576,12,64]{1,3,2,0:T(8,128)}, u32[]{:S(2)}) copy-start(f32[2,576,12,64]{1,3,2,0:T(8,128)} %get-tuple-element.509) | copy-start | bytes 10616836 | tf_op jit(solution)/shard_map/while
  689.5 2.7 copy-start.1
  689.5 2.7 copy-start.13
  692.2 1.9 copy-start.12
  694.1 2.0 copy-start.14
  701.5 1.5 copy-start.10
  733.7 8.2 copy-start.36
  733.7 9.3 copy-start.35
  733.7 13.2 %copy-start.29 = (f32[1152]{0:T(1024)S(1)}, f32[1152]{0:T(1024)}, u32[]{:S(2)}) copy-start(f32[1152]{0:T(1024)} %copy-done.28) | copy-start | bytes 13828
  733.7 13.1 %copy-start.30 = (f32[1152]{0:T(1024)S(1)}, f32[1152]{0:T(1024)}, u32[]{:S(2)}) copy-start(f32[1152]{0:T(1024)} %rsqrt.21) | copy-start | bytes 13828
  939.1 6.6 copy-start.20
  (3 other events, 2.6 us)
Sparse Core Ops, SparseCore 0:
  176.4 53.5 all-gather.2
  232.1 50.8 all-gather.4
  318.1 109.2 all-reduce.7
  430.0 62.6 reduce-scatter.4
  495.1 63.7 reduce-scatter.2
  733.8 192.4 all-reduce.5
where the time goes:
time: 964 us; the launch traced here: 957 us
  waiting for transfers between devices  370 us (38%)
  matrix products  231 us (24%)
  other arithmetic  145 us (15%)
  local copies, waits for them, and re-layouts  122 us (13%)
  blocking collectives  64 us (7%)
  between operations  23.8 us (2%)
    psum x1, waiting for transfers between devices, body(): lax.psum((ln1_gain_grad, ln1_bias_grad, qkv_weight_grad, qkv_bias_grad, f...  106 us
    reduce_scatter x1, waiting for transfers between devices, body(): lax.psum_scatter(contract_cols(piece, fc1_weight).astype(jnp.bfloat16), '...  60.7 us
    reduce_scatter x1, waiting for transfers between devices, body(): lax.psum_scatter(jnp.dot(piece, fc2_weight, preferred_element_type=jnp.fl...  60.3 us
    psum x1, waiting for transfers between devices, body(): lax.psum(fc1_weight_grad.astype(jnp.bfloat16), 'dp').astype(jnp.float32)  56.7 us
    all_gather x1, waiting for transfers between devices, body(): all_normed = lax.all_gather(normed_two, 'tensor', axis=0, tiled=True)  47.9 us
    dot_general x4, matrix products, masked_scores(): jnp.einsum('qhd,khd->hqk', queries, key_rows, preferred_element_type=jnp....  44.3 us
    psum x1, blocking collectives, body(): lax.psum((ln1_gain_grad, ln1_bias_grad, qkv_weight_grad, qkv_bias_grad, f...  41.8 us
    all_gather x1, waiting for transfers between devices, body(): all_grads = lax.all_gather(low_grad_rows, 'tensor', axis=0, tiled=True)  38.8 us
  transfers between devices with their start and end apart: 6, of which 6 were waited for; matrix products, arithmetic and copies ran while one was open for 11% of the time, Pallas kernels for 0%

commit v1 on v0

v1 whole, which is shorter than its diff:
```python
import functools

import jax
import jax.numpy as jnp
from jax import lax
from jax.experimental import pallas as pl
from jax.experimental.pallas import tpu as pltpu
from jax.sharding import PartitionSpec as P

GRID = 24
EPSILON = 1e-06
MASKED_SCORE = -1e30
ROOT_HALF = 0.7071067811865476
DENSITY_SCALE = 0.3989422804014327
F32 = jnp.float32
BF16 = jnp.bfloat16
LANES = 128
HEAD = 64
GROUPS = 3
VMEM_LIMIT = 56 << 20


def dot(left, right, left_dim=1, right_dim=0):
    return lax.dot_general(
        left, right, (((left_dim,), (right_dim,)), ((), ())), preferred_element_type=F32
    )


def normalize(row_data):
    row_mean = jnp.mean(row_data, axis=-1, keepdims=True)
    centred = row_data - row_mean
    inverse = lax.rsqrt(jnp.mean(centred * centred, axis=-1, keepdims=True) + EPSILON)
    return (centred * inverse, inverse)


def norm_back(grad_unit, unit_rows, inverse):
    return inverse * (
        grad_unit
        - jnp.mean(grad_unit, axis=-1, keepdims=True)
        - unit_rows * jnp.mean(grad_unit * unit_rows, axis=-1, keepdims=True)
    )


def gelu_exact(values):
    return 0.5 * values * (1.0 + lax.erf(values * ROOT_HALF))


def gelu_slope(values):
    return (
        0.5 * (1.0 + lax.erf(values * ROOT_HALF))
        + values * jnp.exp(-0.5 * values * values) * DENSITY_SCALE
    )


def swap_halves(tile):
    lane = lax.broadcasted_iota(jnp.int32, (1, LANES), 1)
    first = (lane % HEAD) < HEAD // 2
    return jnp.where(
        first, pltpu.roll(tile, LANES - HEAD // 2, 1), pltpu.roll(tile, HEAD // 2, 1)
    )


def qkv_kernel(
    x_ref, gain_ref, shift_ref, weight_ref, bias_ref, cos_ref, sin_ref, normed_ref, qkv_ref
):
    width = x_ref.shape[1]
    unit, _ = normalize(x_ref[...].astype(F32))
    normed = (unit * gain_ref[...] + shift_ref[...]).astype(BF16)
    normed_ref[...] = normed
    for part in range(3):
        packed = (
            dot(normed, weight_ref[:, part * width : (part + 1) * width])
            + bias_ref[:, part * width : (part + 1) * width]
        )
        for tile in range(width // LANES):
            cols = slice(tile * LANES, (tile + 1) * LANES)
            piece = packed[:, cols]
            if part < 2:
                piece = piece * cos_ref[:, cols] + swap_halves(piece) * sin_ref[:, cols]
            if part == 0:
                piece = piece * (HEAD**-0.5)
            qkv_ref[:, part * width + tile * LANES : part * width + (tile + 1) * LANES] = (
                piece.astype(BF16)
            )


def project_qkv(rows, gain, shift, weight, bias, cosine, sine, slots):
    row_count, width = rows.shape
    tile = slots // 2
    whole = lambda shape: pl.BlockSpec(shape, lambda i: (0, 0))
    return pl.pallas_call(
        qkv_kernel,
        grid=(row_count // tile,),
        in_specs=[
            pl.BlockSpec((tile, width), lambda i: (i, 0)),
            whole((1, width)),
            whole((1, width)),
            whole((width, 3 * width)),
            whole((1, 3 * width)),
            pl.BlockSpec((tile, width), lambda i: (i % 2, 0)),
            pl.BlockSpec((tile, width), lambda i: (i % 2, 0)),
        ],
        out_specs=[
            pl.BlockSpec((tile, width), lambda i: (i, 0)),
            pl.BlockSpec((tile, 3 * width), lambda i: (i, 0)),
        ],
        out_shape=[
            jax.ShapeDtypeStruct((row_count, width), BF16),
            jax.ShapeDtypeStruct((row_count, 3 * width), BF16),
        ],
        cost_estimate=pl.CostEstimate(
            flops=6 * row_count * width * width,
            bytes_accessed=row_count * width * 16 + 6 * width * width,
            transcendentals=0,
        ),
        compiler_params=pltpu.CompilerParams(vmem_limit_bytes=VMEM_LIMIT),
    )(rows, gain, shift, weight, bias, cosine, sine)


def attend_kernel(q_ref, k_ref, v_ref, mask_ref, mixed_ref, total_ref):
    low = lax.broadcasted_iota(jnp.int32, (1, LANES), 1) < HEAD
    queries, keys, values = q_ref[...], k_ref[...], v_ref[...]
    zero = jnp.zeros_like(queries)
    mask = mask_ref[0]
    mixed, totals = None, []
    for head in range(2):
        keep = low if head == 0 else ~low
        scores = dot(jnp.where(keep, queries, zero), keys, 1, 1) + mask
        row_max = jnp.max(scores, axis=1, keepdims=True)
        weights = jnp.exp(scores - row_max)
        row_total = jnp.sum(weights, axis=1, keepdims=True)
        low_weights = (weights * (1.0 / row_total)).astype(BF16)
        part = dot(low_weights, jnp.where(keep, values, zero))
        mixed = part if mixed is None else mixed + part
        totals.append(row_max + jnp.log(row_total))
    mixed_ref[...] = mixed.astype(BF16)
    total_ref[...] = jnp.where(low, totals[0], totals[1])


def attend(qkv, mask_row, slots):
    row_count, width = qkv.shape[0], qkv.shape[1] // 3
    images, pairs = row_count // slots, width // LANES
    block = lambda part: pl.BlockSpec((slots, LANES), lambda i, p: (i, p + part * pairs))
    return pl.pallas_call(
        attend_kernel,
        grid=(images, pairs),
        in_specs=[
            block(0),
            block(1),
            block(2),
            pl.BlockSpec((1, 1, slots), lambda i, p: (i, 0, 0)),
        ],
        out_specs=[block(0), block(0)],
        out_shape=[
            jax.ShapeDtypeStruct((row_count, width), BF16),
            jax.ShapeDtypeStruct((row_count, width), F32),
        ],
        cost_estimate=pl.CostEstimate(
            flops=16 * row_count * slots * width,
            bytes_accessed=row_count * width * 12,
            transcendentals=row_count * slots * 2 * pairs,
        ),
        compiler_params=pltpu.CompilerParams(vmem_limit_bytes=VMEM_LIMIT),
    )(qkv, qkv, qkv, mask_row)


def attend_back_pair(q, k, v, mixed, grad_mixed, totals, mask, cosine, sine, place):
    low = lax.broadcasted_iota(jnp.int32, (1, LANES), 1) < HEAD
    zero = jnp.zeros_like(q)
    product = jnp.transpose(grad_mixed.astype(F32) * mixed.astype(F32))
    totals = jnp.transpose(totals)
    grad_q = grad_k = grad_v = None
    for head in range(2):
        keep = low if head == 0 else ~low
        q_head = jnp.where(keep, q, zero)
        grad_head = jnp.where(keep, grad_mixed, zero)
        k_head = jnp.where(keep, k, zero)
        total = totals[head * HEAD : head * HEAD + 1]
        inner = jnp.sum(product[head * HEAD : (head + 1) * HEAD], axis=0, keepdims=True)
        weights = jnp.exp((dot(k, q_head, 1, 1) + mask) - total)
        grad_weights = dot(v, grad_head, 1, 1)
        grad_scores = (weights * (grad_weights - inner)).astype(BF16)
        part_v = dot(weights.astype(BF16), grad_head)
        part_k = dot(grad_scores, q_head)
        part_q = dot(grad_scores, k_head, 0, 0)
        grad_v = part_v if grad_v is None else grad_v + part_v
        grad_k = part_k if grad_k is None else grad_k + part_k
        grad_q = part_q if grad_q is None else grad_q + part_q
    turn = grad_q * swap_halves(q.astype(F32)) + grad_k * swap_halves(k.astype(F32))
    freq_across = jnp.sum(turn * place[:, 0:1], axis=0, keepdims=True)
    freq_down = jnp.sum(turn * place[:, 1:2], axis=0, keepdims=True)
    grad_q = grad_q * (HEAD**-0.5)
    grad_q = (grad_q * cosine - swap_halves(grad_q) * sine).astype(BF16)
    grad_k = (grad_k * cosine - swap_halves(grad_k) * sine).astype(BF16)
    return (grad_q, grad_k, grad_v.astype(BF16), freq_across, freq_down)


def attend_back_kernel(
    q_ref, k_ref, v_ref, mixed_ref, grad_ref, total_ref, mask_ref, cos_ref, sin_ref, place_ref,
    packed_ref, sums_ref,
):
    span = q_ref.shape[1]
    row = lax.broadcasted_iota(jnp.int32, (8, LANES), 0)
    for pair in range(span // LANES):
        cols = slice(pair * LANES, (pair + 1) * LANES)
        grad_q, grad_k, grad_v, across, down = attend_back_pair(
            q_ref[:, cols], k_ref[:, cols], v_ref[:, cols], mixed_ref[:, cols], grad_ref[:, cols],
            total_ref[:, cols], mask_ref[...], cos_ref[:, cols], sin_ref[:, cols], place_ref[...],
        )
        sums = jnp.where(row == 0, across, jnp.where(row == 1, down, 0.0))
        for part, member in enumerate((grad_q, grad_k, grad_v)):
            packed_ref[:, part * span + pair * LANES : part * span + (pair + 1) * LANES] = member
            column_sum = jnp.sum(member.astype(F32), axis=0, keepdims=True)
            sums = jnp.where(row == 2 + part, column_sum, sums)
        sums_ref[0, :, cols] = sums


def attend_back(qkv, mixed, grad_mixed, totals, mask_col, cosine, sine, place, slots, group):
    row_count, width = mixed.shape
    images, span = row_count // slots, width // GROUPS
    block = lambda part: pl.BlockSpec((slots, span), lambda i: (i, group + part * GROUPS))
    table = pl.BlockSpec((slots, span), lambda i: (0, group))
    pairs = span // LANES
    return pl.pallas_call(
        attend_back_kernel,
        grid=(images,),
        in_specs=[
            block(0), block(1), block(2), block(0), block(0), block(0),
            pl.BlockSpec((slots, 1), lambda i: (i, 0)),
            table,
            table,
            pl.BlockSpec((slots, LANES), lambda i: (0, 0)),
        ],
        out_specs=[
            pl.BlockSpec((slots, 3 * span), lambda i: (i, 0)),
            pl.BlockSpec((1, 8, span), lambda i: (i, 0, 0)),
        ],
        out_shape=[
            jax.ShapeDtypeStruct((row_count, 3 * span), BF16),
            jax.ShapeDtypeStruct((images, 8, span), F32),
        ],
        cost_estimate=pl.CostEstimate(
            flops=40 * row_count * slots * span,
            bytes_accessed=row_count * span * 20,
            transcendentals=row_count * slots * 2 * pairs,
        ),
        compiler_params=pltpu.CompilerParams(vmem_limit_bytes=VMEM_LIMIT),
    )(qkv, qkv, qkv, mixed, grad_mixed, totals, mask_col, cosine, sine, place)


class Exchange:
    def __init__(self, mesh):
        self.sizes = dict(mesh.shape)

    def bits(self, axis):
        return [(axis, 1 << b) for b in range(self.sizes[axis].bit_length() - 1)]

    def swap(self, value, step):
        axis, bit = step
        pairs = [(i, i ^ bit) for i in range(self.sizes[axis])]
        return lax.ppermute(value, axis, pairs)

    def side(self, step):
        axis, bit = step
        return (lax.axis_index(axis) // bit) % 2

    def halve(self, value, step):
        size = value.shape[0] // 2
        mine = self.side(step)
        keep = lax.dynamic_slice_in_dim(value, mine * size, size, 0)
        send = lax.dynamic_slice_in_dim(value, (1 - mine) * size, size, 0)
        got = self.swap(send, step)
        return (keep.astype(F32) + got.astype(F32)).astype(BF16)

    def double(self, value, step):
        other = self.swap(value, step)
        first = self.side(step) == 0
        return jnp.concatenate(
            [jnp.where(first, value, other), jnp.where(first, other, value)], axis=0
        )

    def sum_over(self, value, steps):
        for step in steps:
            value = self.halve(value, step)
        for step in reversed(steps):
            value = self.double(value, step)
        return value

    def sum_small(self, value, steps):
        for step in steps:
            value = value + self.swap(value, step)
        return value


def body(
    net,
    images,
    keep_mask,
    ln1_gain,
    ln1_bias,
    qkv_weight,
    qkv_bias,
    frequencies,
    proj_weight,
    proj_bias,
    ln2_gain,
    ln2_bias,
    fc1_weight,
    fc1_bias,
    fc2_weight,
    fc2_bias,
    out_grad,
):
    image_count, slots, width = images.shape
    row_count = image_count * slots
    span = width // GROUPS
    inner_step, outer_step = net.bits("tensor")
    tensor_steps, dp_steps = net.bits("tensor"), net.bits("dp")

    shards = {0: (fc1_weight, fc1_bias, fc2_weight)}
    shards[2] = tuple(net.swap(member, outer_step) for member in shards[0])
    shards[1] = tuple(net.swap(member, inner_step) for member in shards[0])
    shards[3] = tuple(net.swap(member, inner_step) for member in shards[2])

    kept = keep_mask.astype(F32)
    kept_col = kept.reshape(row_count, 1)
    mask_add = jnp.where(kept > 0, 0.0, MASKED_SCORE)
    mask_row = mask_add.reshape(image_count, 1, slots)
    mask_col = mask_add.reshape(row_count, 1)
    place = jnp.arange(slots)
    across = (place // GRID).astype(F32)
    downward = (place % GRID).astype(F32)
    lane_freq = jnp.concatenate([frequencies, frequencies], axis=-1).reshape(2, 1, width)
    steps = jnp.arange(slots // GRID).astype(F32)[:, None]
    angle_a = steps * lane_freq[0]
    angle_d = jnp.arange(GRID).astype(F32)[:, None] * lane_freq[1]
    sign = jnp.where(jnp.arange(width) % HEAD < HEAD // 2, -1.0, 1.0)
    cos_a, sin_a = jnp.cos(angle_a)[:, None], jnp.sin(angle_a)[:, None]
    cos_d, sin_d = jnp.cos(angle_d)[None], jnp.sin(angle_d)[None]
    cosine = (cos_a * cos_d - sin_a * sin_d).reshape(slots, width)
    sine = ((sin_a * cos_d + cos_a * sin_d) * sign).reshape(slots, width)
    lane = jnp.arange(LANES)[None]
    places = jnp.where(lane == 0, across[:, None], jnp.where(lane == 1, downward[:, None], 0.0))

    rows = images.reshape(row_count, width)
    row_of = lambda vector: vector.reshape(1, -1)
    normed_one, qkv = project_qkv(
        rows, row_of(ln1_gain), row_of(ln1_bias), qkv_weight, row_of(qkv_bias), cosine, sine, slots
    )
    mixed, totals = attend(qkv, mask_row, slots)

    inputs = rows.astype(F32)
    resid = inputs + dot(mixed, proj_weight) + proj_bias
    unit_two, inverse_two = normalize(resid)
    normed_two = (unit_two * ln2_gain + ln2_bias).astype(BF16)
    grad_low = (kept_col * out_grad.astype(F32).reshape(row_count, width)).astype(BF16)

    mlp_out = jnp.zeros((), F32)
    grad_normed_two = jnp.zeros((), F32)
    fc1_grads, fc2_grads, hidden_sums = {}, {}, {}
    for r in (0, 2, 3, 1):
        weight_in, bias_in, weight_out = shards[r]
        hidden = dot(normed_two, weight_in) + bias_in.astype(F32)
        active = gelu_exact(hidden).astype(BF16)
        mlp_out = mlp_out + dot(active, weight_out)
        fc2_grads[r] = dot(active, grad_low, 0, 0).astype(BF16)
        grad_hidden = (dot(grad_low, weight_out, 1, 1) * gelu_slope(hidden)).astype(BF16)
        fc1_grads[r] = dot(normed_two, grad_hidden, 0, 0).astype(BF16)
        hidden_sums[r] = jnp.sum(grad_hidden.astype(F32), axis=0)
        grad_normed_two = grad_normed_two + dot(grad_hidden, weight_in, 1, 1)

    def to_owner(grads, order):
        far = grads[2].astype(F32) + net.swap(grads[3], inner_step).astype(F32)
        far = net.swap(far.astype(BF16), outer_step)
        near = grads[0].astype(F32) + net.swap(grads[1], inner_step).astype(F32)
        return net.sum_over((near + far.astype(F32)).astype(BF16), order)

    rotated = dp_steps[1:] + dp_steps[:1]
    fc2_weight_grad = to_owner(fc2_grads, dp_steps).astype(F32)
    fc1_weight_grad = to_owner(fc1_grads, rotated).astype(F32)

    grad_rows = grad_low.astype(F32)
    block_out = (kept_col * (resid + mlp_out + fc2_bias)).astype(BF16).reshape(images.shape)
    grad_resid = grad_rows + norm_back(grad_normed_two * ln2_gain, unit_two, inverse_two)
    low_grad_branch = grad_resid.astype(BF16)
    proj_weight_grad = dot(mixed, low_grad_branch, 0, 0).astype(BF16)
    low_grad_mixed = dot(low_grad_branch, proj_weight, 1, 1).astype(BF16)
    proj_weight_grad = net.sum_over(proj_weight_grad, tensor_steps + dp_steps).astype(F32)

    own = lax.axis_index("tensor")
    parts = jnp.arange(4)[:, None]
    hidden_rows = sum(jnp.where(parts == (own ^ r), hidden_sums[r][None], 0.0) for r in range(4))
    early = jnp.concatenate(
        [
            hidden_rows,
            jnp.stack(
                [
                    jnp.sum(low_grad_branch.astype(F32), axis=0),
                    jnp.sum(grad_normed_two * unit_two, axis=0),
                    jnp.sum(grad_normed_two, axis=0),
                    jnp.sum(grad_rows, axis=0),
                ]
            ),
        ],
        axis=0,
    )
    early = net.sum_small(early, tensor_steps + dp_steps)
    fc1_bias_grad = lax.dynamic_slice_in_dim(early, own, 1, 0)[0]
    proj_bias_grad, ln2_gain_grad, ln2_bias_grad, fc2_bias_grad = early[4:]

    grad_normed_one = jnp.zeros((), F32)
    group_grads, group_sums = [], []
    orders = [tensor_steps + dp_steps, dp_steps + tensor_steps, tensor_steps + rotated]
    for group in range(GROUPS):
        packed, sums = attend_back(
            qkv, mixed, low_grad_mixed, totals, mask_col, cosine, sine, places, slots, group
        )
        group_sums.append(jnp.sum(sums, axis=0))
        weight_grad = dot(normed_one, packed, 0, 0).astype(BF16)
        group_grads.append(net.sum_over(weight_grad, orders[group]).astype(F32))
        weight = jnp.concatenate(
            [
                qkv_weight[:, part * width + group * span : part * width + (group + 1) * span]
                for part in range(3)
            ],
            axis=1,
        )
        grad_normed_one = grad_normed_one + dot(packed, weight, 1, 1)
    qkv_weight_grad = jnp.concatenate(
        [g[:, part * span : (part + 1) * span] for part in range(3) for g in group_grads], axis=1
    )

    unit_one, inverse_one = normalize(inputs)
    input_grad = grad_resid + norm_back(grad_normed_one * ln1_gain, unit_one, inverse_one)
    input_grad = input_grad.astype(BF16).reshape(images.shape)
    late = jnp.concatenate(
        [
            jnp.concatenate(group_sums, axis=1)[:5],
            jnp.stack(
                [jnp.sum(grad_normed_one * unit_one, axis=0), jnp.sum(grad_normed_one, axis=0)]
            ),
            jnp.zeros((1, width), F32),
        ],
        axis=0,
    )
    late = net.sum_small(late, tensor_steps + dp_steps)
    turned = late[:2].reshape(2, width // HEAD, 2, HEAD // 2)
    freq_grad = turned[:, :, 1] - turned[:, :, 0]
    qkv_bias_grad = late[2:5].reshape(-1)
    ln1_gain_grad, ln1_bias_grad = late[5], late[6]

    freq_norm = jnp.sqrt(jnp.sum(freq_grad * freq_grad))
    square = jnp.float32(0.0)
    for member in (
        ln1_gain_grad,
        ln1_bias_grad,
        qkv_weight_grad,
        qkv_bias_grad,
        proj_weight_grad,
        proj_bias_grad,
        ln2_gain_grad,
        ln2_bias_grad,
        fc2_bias_grad,
    ):
        square = square + jnp.sum(member * member)
    return (
        block_out,
        input_grad,
        ln1_gain_grad,
        ln1_bias_grad,
        qkv_weight_grad,
        qkv_bias_grad,
        freq_grad,
        proj_weight_grad,
        proj_bias_grad,
        ln2_gain_grad,
        ln2_bias_grad,
        fc1_weight_grad,
        fc1_bias_grad,
        fc2_weight_grad,
        fc2_bias_grad,
        freq_norm,
        jnp.sqrt(square),
    )


def solution(mesh):
    rows = P(("dp", "tensor"), None, None)
    whole = P()
    hidden_in, hidden_out = P(None, "tensor"), P("tensor", None)
    return jax.shard_map(
        functools.partial(body, Exchange(mesh)),
        mesh=mesh,
        in_specs=(
            (rows, P(("dp", "tensor"), None))
            + (whole,) * 9
            + (hidden_in, P("tensor"), hidden_out, whole, rows)
        ),
        out_specs=(
            (rows, rows) + (whole,) * 9 + (hidden_in, P("tensor"), hidden_out) + (whole,) * 3
        ),
        check_vma=False,
    )
```

time: 964 us -> 534 us (0.55)
  waiting for transfers between devices: 370 us -> 199 us
  matrix products: 231 us -> 110 us
  other arithmetic: 145 us -> 55.3 us
  local copies, waits for them, and re-layouts: 122 us -> 33.5 us
  Pallas kernels: 0 us -> 73.3 us
  blocking collectives: 64 us -> 0 us
  starting transfers between devices: 0.25 us -> 47.9 us
  between operations: 23.8 us -> 11.5 us
    ppermute x0 -> x77, waiting for transfers between devices: none -> 199 us  [swap(): return lax.ppermute(value, axis, pairs)]
    psum x2 -> x0, waiting for transfers between devices: 163 us -> none  [the longest x1 106 us: body(): lax.psum((ln1_gain_grad, ln1_bias_grad, qkv_weight_grad, qkv_bias_grad, f...]
    reduce_scatter x2 -> x0, waiting for transfers between devices: 121 us -> none  [the longest x1 60.7 us: body(): lax.psum_scatter(contract_cols(piece, fc1_weight).astype(jnp.bfloat16), '...]
    dot_general x28 -> x33, matrix products: 231 us -> 110 us  [dot(): lax.dot_general(left, right, (((left_dim,), (right_dim,)), ((), ())), pre...]
    all_gather x2 -> x0, waiting for transfers between devices: 86.7 us -> none  [the longest x1 47.9 us: body(): all_normed = lax.all_gather(normed_two, 'tensor', axis=0, tiled=True)]
    pallas_call x0 -> x5, Pallas kernels: none -> 73.3 us  [the longest x3 40.4 us: attend_back(): pl.pallas_call(attend_back_kernel, grid=(images,), in_specs=[block(0), bl...]
    psum x2 -> x0, blocking collectives: 64 us -> none  [the longest x1 41.8 us: body(): lax.psum((ln1_gain_grad, ln1_bias_grad, qkv_weight_grad, qkv_bias_grad, f...]
    ppermute x0 -> x77, starting transfers between devices: none -> 47.9 us  [swap(): return lax.ppermute(value, axis, pairs)]
  transfers between devices with their start and end apart: 6 -> 77, of which waited for: 6 -> 43; matrix products, arithmetic and copies ran while one was open for 11% -> 35% of each run, Pallas kernels for 0% -> 14%
where the time goes in v1:
time: 534 us; the launch traced here: 530 us
  waiting for transfers between devices  199 us (37%)
  matrix products  110 us (21%)
  Pallas kernels  73.3 us (14%)
  other arithmetic  55.3 us (10%)
  starting transfers between devices  47.9 us (9%)
  local copies, waits for them, and re-layouts  33.5 us (6%)
  between operations  11.5 us (2%)
    ppermute x77, waiting for transfers between devices, swap(): return lax.ppermute(value, axis, pairs)  199 us
    dot_general x33, matrix products, dot(): lax.dot_general(left, right, (((left_dim,), (right_dim,)), ((), ())), pre...  110 us
    ppermute x77, starting transfers between devices, swap(): return lax.ppermute(value, axis, pairs)  47.9 us
    pallas_call x3, Pallas kernels, attend_back(): pl.pallas_call(attend_back_kernel, grid=(images,), in_specs=[block(0), bl...  40.4 us
    pallas_call x1, Pallas kernels, attend(): pl.pallas_call(attend_kernel, grid=(images, pairs), in_specs=[block(0), b...  21.7 us
    pallas_call x1, Pallas kernels, project_qkv(): pl.pallas_call(qkv_kernel, grid=(row_count // tile,), in_specs=[pl.BlockS...  11.3 us
  transfers between devices with their start and end apart: 77, of which 43 were waited for; matrix products, arithmetic and copies ran while one was open for 35% of the time, Pallas kernels for 14%

profile of v1, /device:TPU:0, one launch (start us, length us, event | category | flops | bytes accessed | tf_op | source)
XLA Modules:
  0.0 529.9 jit_solution(17144989348069383236)
XLA Ops:
  0.7 3.0 collective-permute-start
  12.0 3.9 fusion.82
  19.7 11.3 %shard_map.287 = (bf16[1152,768]{1,0:T(8,128)(2,1)}, bf16[1152,2304]{1,0:T(8,128)(2,1)}) custom-call(bf16[1152,768]{1,0:T(8,128)(2,1)} %bitcast.84, f32[1,768]{1,0:T(1,128)} %reshape.350.gain_ref, f32[1,768]{1,0:T(1,128)} %reshape.351.shift_ref, bf16[768,2304]{1,0:T(8,128)(2,1)} %weight_ref.1, f32[1,2304]{1,0:T(1,128)} %reshape.352.bias_ref, ...), custom_call_target="tpu_custom_call" | custom-call | flops 4076863488 | bytes 17694720 | tf_op jit(solution)/shard_map/pallas_call | solution.py:91
  31.0 21.7 %shard_map.288 = (bf16[1152,768]{1,0:T(8,128)(2,1)}, f32[1152,768]{1,0:T(8,128)}) custom-call(bf16[1152,2304]{1,0:T(8,128)(2,1)} %get-tuple-element.27.q_ref.k_ref.v_ref, bf16[1152,2304]{1,0:T(8,128)(2,1)} %get-tuple-element.27.q_ref.k_ref.v_ref, bf16[1152,2304]{1,0:T(8,128)(2,1)} %get-tuple-element.27.q_ref.k_ref.v_ref, f32[2,1,576]{2,1,0:T(1,128)} %reshape.353.mask_ref), custom_call_target="tpu_custom_call" | custom-call | flops 8153726976 | bytes 10616832 | tf_op jit(solution)/shard_map/pallas_call | solution.py:144
  52.7 3.2 fusion.83
  63.0 4.8 multiply_convert_fusion.4
  67.9 3.3 fusion.84
  74.0 4.5 convert_reduce_fusion.6
  79.8 5.3 %fusion.86 = f32[1152,768]{1,0:T(8,128)} fusion(bf16[1152,768]{1,0:T(8,128)(2,1)} %get-tuple-element.167, bf16[768,768]{1,0:T(8,128)(2,1)} %param.27), kind=kOutput, calls=%fused_computation.344 | convolution fusion | flops 1358954496 | bytes 6488064 | tf_op jit(solution)/shard_map/dot_general | solution.py:24
  85.2 2.8 convolution_convert_fusion.8
  95.0 3.6 multiply_convert_fusion.1
  98.6 2.9 convolution_convert_fusion.3
  101.5 4.6 convert_reduce_fusion.5
  106.1 2.8 convolution_convert_fusion.7
  109.4 4.1 multiply_convert_fusion.3
  113.5 8.0 %collective-permute-done.2 = bf16[768,768]{1,0:T(8,128)(2,1)S(1)} collective-permute-done((bf16[768,768]{1,0:T(8,128)(2,1)}, bf16[768,768]{1,0:T(8,128)(2,1)S(1)}, u32[]{:S(2)}, u32[]{:S(2)}) %collective-permute-start.2) | collective-permute-done | bytes 1179680 | tf_op jit(solution)/shard_map/ppermute | solution.py:261
  121.6 3.4 convert_reduce_fusion.4
  125.0 3.5 convolution_add_fusion.3
  128.5 2.9 fusion.87
  131.4 4.8 fusion.85
  136.2 3.4 convolution_add_fusion.7
  139.6 2.9 multiply_convert_fusion.2
  142.6 3.3 convert_reduce_fusion.3
  145.8 3.2 multiply_reduce_fusion.1
  151.3 2.8 convolution_convert_fusion.grad_ref
  154.1 13.6 %shard_map.291 = (bf16[1152,768]{1,0:T(8,128)(2,1)}, f32[2,8,256]{2,1,0:T(8,128)}) custom-call(bf16[1152,2304]{1,0:T(8,128)(2,1)} %get-tuple-element.27.q_ref.k_ref.v_ref, bf16[1152,2304]{1,0:T(8,128)(2,1)} %get-tuple-element.27.q_ref.k_ref.v_ref, bf16[1152,2304]{1,0:T(8,128)(2,1)} %get-tuple-element.27.q_ref.k_ref.v_ref, ...), custom_call_target="tpu_custom_call" | custom-call | flops 6794772480 | bytes 5898240 | tf_op jit(solution)/shard_map/pallas_call | solution.py:224
  167.7 13.2 %shard_map.290 = (bf16[1152,768]{1,0:T(8,128)(2,1)}, f32[2,8,256]{2,1,0:T(8,128)}) custom-call(bf16[1152,2304]{1,0:T(8,128)(2,1)} %get-tuple-element.27.q_ref.k_ref.v_ref, bf16[1152,2304]{1,0:T(8,128)(2,1)} %get-tuple-element.27.q_ref.k_ref.v_ref, bf16[1152,2304]{1,0:T(8,128)(2,1)} %get-tuple-element.27.q_ref.k_ref.v_ref, ...), custom_call_target="tpu_custom_call" | custom-call | flops 6794772480 | bytes 5898240 | tf_op jit(solution)/shard_map/pallas_call | solution.py:224
  181.0 13.5 %shard_map.289 = (bf16[1152,768]{1,0:T(8,128)(2,1)}, f32[2,8,256]{2,1,0:T(8,128)}) custom-call(bf16[1152,2304]{1,0:T(8,128)(2,1)} %get-tuple-element.27.q_ref.k_ref.v_ref, bf16[1152,2304]{1,0:T(8,128)(2,1)} %get-tuple-element.27.q_ref.k_ref.v_ref, bf16[1152,2304]{1,0:T(8,128)(2,1)} %get-tuple-element.27.q_ref.k_ref.v_ref, ...), custom_call_target="tpu_custom_call" | custom-call | flops 6794772480 | bytes 5898240 | tf_op jit(solution)/shard_map/pallas_call | solution.py:224
  197.3 2.8 convolution_convert_fusion.5
  202.9 2.8 convolution_convert_fusion.11
  205.7 2.8 convolution_convert_fusion.12
  211.9 5.1 fusion.15
  224.2 4.4 convolution_convert_fusion.1
  233.5 4.4 fusion.35
  280.3 12.0 %collective-permute-done.15 = bf16[192,768]{1,0:T(8,128)(2,1)S(1)} collective-permute-done((bf16[192,768]{1,0:T(8,128)(2,1)S(1)}, bf16[192,768]{1,0:T(8,128)(2,1)S(1)}, u32[]{:S(2)}, u32[]{:S(2)}) %collective-permute-start.15) | collective-permute-done | bytes 294944 | tf_op jit(solution)/shard_map/ppermute | solution.py:261
  293.8 7.1 %collective-permute-done.45 = bf16[192,768]{1,0:T(8,128)(2,1)S(1)} collective-permute-done((bf16[192,768]{1,0:T(8,128)(2,1)S(1)}, bf16[192,768]{1,0:T(8,128)(2,1)S(1)}, u32[]{:S(2)}, u32[]{:S(2)}) %collective-permute-start.45) | collective-permute-done | bytes 294944 | tf_op jit(solution)/shard_map/ppermute | solution.py:261
  302.7 5.7 %collective-permute-done.25 = bf16[192,768]{1,0:T(8,128)(2,1)S(1)} collective-permute-done((bf16[192,768]{1,0:T(8,128)(2,1)S(1)}, bf16[192,768]{1,0:T(8,128)(2,1)S(1)}, u32[]{:S(2)}, u32[]{:S(2)}) %collective-permute-start.25) | collective-permute-done | bytes 294944 | tf_op jit(solution)/shard_map/ppermute | solution.py:261
  309.6 4.8 collective-permute-done.16
  315.5 4.1 collective-permute-done.46
  321.2 4.7 collective-permute-done.36
  326.7 6.6 %collective-permute-done.26 = bf16[96,768]{1,0:T(8,128)(2,1)S(1)} collective-permute-done((bf16[96,768]{1,0:T(8,128)(2,1)S(1)}, bf16[96,768]{1,0:T(8,128)(2,1)S(1)}, u32[]{:S(2)}, u32[]{:S(2)}) %collective-permute-start.26) | collective-permute-done | bytes 147488 | tf_op jit(solution)/shard_map/ppermute | solution.py:261
  333.4 4.4 collective-permute-done.17
  337.8 4.3 collective-permute-done.47
  342.2 5.5 %collective-permute-done.37 = bf16[48,768]{1,0:T(8,128)(2,1)S(1)} collective-permute-done((bf16[48,768]{1,0:T(8,128)(2,1)S(1)}, bf16[48,768]{1,0:T(8,128)(2,1)S(1)}, u32[]{:S(2)}, u32[]{:S(2)}) %collective-permute-start.37) | collective-permute-done | bytes 73760 | tf_op jit(solution)/shard_map/ppermute | solution.py:261
  349.0 4.8 collective-permute-done.18
  353.8 4.8 collective-permute-done.48
  373.0 3.0 collective-permute-start.49
  377.9 4.6 collective-permute-done.40
  384.7 4.5 collective-permute-done.20
  390.8 3.5 collective-permute-done.41
  394.4 3.6 collective-permute-done.31
  399.5 3.6 collective-permute-done.51
  403.2 4.5 collective-permute-done.42
  410.6 5.1 collective-permute-done.22
  415.9 2.9 collective-permute-done.52
  422.2 14.0 %collective-permute-done.33 = bf16[384,768]{1,0:T(8,128)(2,1)S(1)} collective-permute-done((bf16[384,768]{1,0:T(8,128)(2,1)S(1)}, bf16[384,768]{1,0:T(8,128)(2,1)S(1)}, u32[]{:S(2)}, u32[]{:S(2)}) %collective-permute-start.33) | collective-permute-done | bytes 589856 | tf_op jit(solution)/shard_map/ppermute | solution.py:261
  442.2 5.2 collective-permute-done.61
  451.8 5.5 %collective-permute-done.71 = bf16[384,768]{1,0:T(8,128)(2,1)S(1)} collective-permute-done((bf16[384,768]{1,0:T(8,128)(2,1)S(1)}, bf16[384,768]{1,0:T(8,128)(2,1)S(1)}, u32[]{:S(2)}, u32[]{:S(2)}) %collective-permute-start.71) | collective-permute-done | bytes 589856 | tf_op jit(solution)/shard_map/ppermute | solution.py:261
  457.5 8.1 %collective-permute-done.62 = bf16[384,768]{1,0:T(8,128)(2,1)S(1)} collective-permute-done((bf16[384,768]{1,0:T(8,128)(2,1)S(1)}, bf16[384,768]{1,0:T(8,128)(2,1)S(1)}, u32[]{:S(2)}, u32[]{:S(2)}) %collective-permute-start.62) | collective-permute-done | bytes 589856 | tf_op jit(solution)/shard_map/ppermute | solution.py:261
  465.8 7.8 %collective-permute-done.72 = bf16[192,768]{1,0:T(8,128)(2,1)S(1)} collective-permute-done((bf16[192,768]{1,0:T(8,128)(2,1)S(1)}, bf16[192,768]{1,0:T(8,128)(2,1)S(1)}, u32[]{:S(2)}, u32[]{:S(2)}) %collective-permute-start.72) | collective-permute-done | bytes 294944 | tf_op jit(solution)/shard_map/ppermute | solution.py:261
  474.6 9.7 %collective-permute-done.63 = bf16[192,768]{1,0:T(8,128)(2,1)S(1)} collective-permute-done((bf16[192,768]{1,0:T(8,128)(2,1)S(1)}, bf16[192,768]{1,0:T(8,128)(2,1)S(1)}, u32[]{:S(2)}, u32[]{:S(2)}) %collective-permute-start.63) | collective-permute-done | bytes 294944 | tf_op jit(solution)/shard_map/ppermute | solution.py:261
  486.0 4.4 collective-permute-done.64
  495.8 9.8 %collective-permute-done.75 = bf16[192,768]{1,0:T(8,128)(2,1)S(1)} collective-permute-done((bf16[192,768]{1,0:T(8,128)(2,1)S(1)}, bf16[192,768]{1,0:T(8,128)(2,1)S(1)}, u32[]{:S(2)}, u32[]{:S(2)}) %collective-permute-start.75) | collective-permute-done | bytes 294944 | tf_op jit(solution)/shard_map/ppermute | solution.py:261
  516.4 4.6 collective-permute-done.76
  (496 shorter events, 162.4 us)
Async XLA Ops:
  0.7 108.7 %collective-permute-start = (bf16[768,768]{1,0:T(8,128)(2,1)}, bf16[768,768]{1,0:T(8,128)(2,1)}, u32[]{:S(2)}, u32[]{:S(2)}) collective-permute-start(bf16[768,768]{1,0:T(8,128)(2,1)} %param.27), channel_id=1, source_target_pairs={{0,2},{1,3},{2,0},{3,1},{4,6},{5,7},{6,4},{7,5},{8,10},{9,11},{10,... | collective-permute-start | bytes 3538952 | tf_op jit(solution)/shard_map/ppermute | solution.py:261
  3.7 91.3 %collective-permute-start.6 = (bf16[768,768]{1,0:T(8,128)(2,1)}, bf16[768,768]{1,0:T(8,128)(2,1)}, u32[]{:S(2)}, u32[]{:S(2)}) collective-permute-start(bf16[768,768]{1,0:T(8,128)(2,1)} %param.27), channel_id=1, source_target_pairs={{0,1},{1,0},{2,3},{3,2},{4,5},{5,4},{6,7},{7,6},{8,9},{9,8},{10,11... | collective-permute-start | bytes 3538952 | tf_op jit(solution)/shard_map/ppermute | solution.py:261
  3.7 89.2 %collective-permute-start.1 = (bf16[768]{0:T(1024)(128)(2,1)}, bf16[768]{0:T(1024)(128)(2,1)S(1)}, u32[]{:S(2)}, u32[]{:S(2)}) collective-permute-start(bf16[768]{0:T(1024)(128)(2,1)} %param.28), channel_id=1, source_target_pairs={{0,2},{1,3},{2,0},{3,1},{4,6},{5,7},{6,4},{7,5},{8,10},{9,11},{10,... | collective-permute-start | bytes 4616 | tf_op jit(solution)/shard_map/ppermute | solution.py:261
  3.9 89.3 %collective-permute-start.7 = (bf16[768]{0:T(1024)(128)(2,1)}, bf16[768]{0:T(1024)(128)(2,1)S(1)}, u32[]{:S(2)}, u32[]{:S(2)}) collective-permute-start(bf16[768]{0:T(1024)(128)(2,1)} %param.28), channel_id=1, source_target_pairs={{0,1},{1,0},{2,3},{3,2},{4,5},{5,4},{6,7},{7,6},{8,9},{9,8},{10,11... | collective-permute-start | bytes 4616 | tf_op jit(solution)/shard_map/ppermute | solution.py:261
  4.2 97.3 %collective-permute-start.8 = (bf16[768,768]{1,0:T(8,128)(2,1)}, bf16[768,768]{1,0:T(8,128)(2,1)}, u32[]{:S(2)}, u32[]{:S(2)}) collective-permute-start(bf16[768,768]{1,0:T(8,128)(2,1)} %param.29), channel_id=1, source_target_pairs={{0,1},{1,0},{2,3},{3,2},{4,5},{5,4},{6,7},{7,6},{8,9},{9,8},{10,11... | collective-permute-start | bytes 3538952 | tf_op jit(solution)/shard_map/ppermute | solution.py:261
  93.2 28.4 %collective-permute-start.2 = (bf16[768,768]{1,0:T(8,128)(2,1)}, bf16[768,768]{1,0:T(8,128)(2,1)S(1)}, u32[]{:S(2)}, u32[]{:S(2)}) collective-permute-start(bf16[768,768]{1,0:T(8,128)(2,1)} %param.29), channel_id=1, source_target_pairs={{0,2},{1,3},{2,0},{3,1},{4,6},{5,7},{6,4},{7,5},{8,10},{9,11},{10,... | collective-permute-start | bytes 3538952 | tf_op jit(solution)/shard_map/ppermute | solution.py:261
  101.5 335.6 %collective-permute-start.68 = (bf16[768,768]{1,0:T(8,128)(2,1)}, bf16[768,768]{1,0:T(8,128)(2,1)}, u32[]{:S(2)}, u32[]{:S(2)}) collective-permute-start(bf16[768,768]{1,0:T(8,128)(2,1)} %convolution_convert_fusion.3), channel_id=1, source_target_pairs={{0,1},{1,0},{2,3},{3,2},{4,5},{5,4},{6,7},{7,6},{8,9},{9,8},{10,11... | collective-permute-start | bytes 3538952 | tf_op jit(solution)/shard_map/ppermute | solution.py:261
  108.9 333.3 %collective-permute-start.59 = (bf16[768,768]{1,0:T(8,128)(2,1)}, bf16[768,768]{1,0:T(8,128)(2,1)}, u32[]{:S(2)}, u32[]{:S(2)}) collective-permute-start(bf16[768,768]{1,0:T(8,128)(2,1)} %convolution_convert_fusion.7), channel_id=1, source_target_pairs={{0,1},{1,0},{2,3},{3,2},{4,5},{5,4},{6,7},{7,6},{8,9},{9,8},{10,11... | collective-permute-start | bytes 3538952 | tf_op jit(solution)/shard_map/ppermute | solution.py:261
  109.4 30.2 %collective-permute-start.3 = (bf16[768,768]{1,0:T(8,128)(2,1)}, bf16[768,768]{1,0:T(8,128)(2,1)S(1)}, u32[]{:S(2)}, u32[]{:S(2)}) collective-permute-start(bf16[768,768]{1,0:T(8,128)(2,1)} %collective-permute-done), channel_id=1, source_target_pairs={{0,1},{1,0},{2,3},{3,2},{4,5},{5,4},{6,7},{7,6},{8,9},{9,8},{10,11... | collective-permute-start | bytes 3538952 | tf_op jit(solution)/shard_map/ppermute | solution.py:261
  121.6 21.0 %collective-permute-start.5 = (bf16[768,768]{1,0:T(8,128)(2,1)S(1)}, bf16[768,768]{1,0:T(8,128)(2,1)S(1)}, u32[]{:S(2)}, u32[]{:S(2)}) collective-permute-start(bf16[768,768]{1,0:T(8,128)(2,1)S(1)} %collective-permute-done.2), channel_id=1, source_target_pairs={{0,1},{1,0},{2,3},{3,2},{4,5},{5,4},{6,7},{7,6},{8,9},{9,8},{10,11... | collective-permute-start | bytes 3538952 | tf_op jit(solution)/shard_map/ppermute | solution.py:261
  223.6 15.2 %collective-permute-start.9 = (f32[8,768]{1,0:T(8,128)}, f32[8,768]{1,0:T(8,128)}, u32[]{:S(2)}, u32[]{:S(2)}) collective-permute-start(f32[8,768]{1,0:T(8,128)} %fusion.58), channel_id=1, source_target_pairs={{0,1},{1,0},{2,3},{3,2},{4,5},{5,4},{6,7},{7,6},{8,9},{9,8},{10,11... | collective-permute-start | bytes 73736 | tf_op jit(solution)/shard_map/ppermute | solution.py:261
  242.5 32.0 %collective-permute-start.34 = (bf16[384,768]{1,0:T(8,128)(2,1)S(1)}, bf16[384,768]{1,0:T(8,128)(2,1)}, u32[]{:S(2)}, u32[]{:S(2)}) collective-permute-start(bf16[384,768]{1,0:T(8,128)(2,1)S(1)} %constant_dynamic-slice_fusion.16), channel_id=1, source_target_pairs={{0,1},{1,0},{2,3},{3,2},{4,5},{5,4},{6,7},{7,6},{8,9},{9,8},{10,11... | collective-permute-start | bytes 1769480 | tf_op jit(solution)/shard_map/ppermute | solution.py:261
  243.9 4.9 collective-permute-start.11
  247.6 4.8 collective-permute-start.56
  253.1 5.3 collective-permute-start.13
  256.6 21.7 %collective-permute-start.24 = (bf16[384,768]{1,0:T(8,128)(2,1)}, bf16[384,768]{1,0:T(8,128)(2,1)}, u32[]{:S(2)}, u32[]{:S(2)}) collective-permute-start(bf16[384,768]{1,0:T(8,128)(2,1)} %constant_dynamic-slice_fusion.21), channel_id=1, source_target_pairs={{0,4},{4,0},{8,12},{12,8},{16,20},{20,16},{24,28},{28,24},{1,5},{5... | collective-permute-start | bytes 1769480 | tf_op jit(solution)/shard_map/ppermute | solution.py:261
  258.3 12.0 %collective-permute-start.58 = (f32[8,768]{1,0:T(8,128)}, f32[8,768]{1,0:T(8,128)}, u32[]{:S(2)}, u32[]{:S(2)}) collective-permute-start(f32[8,768]{1,0:T(8,128)} %add.617), channel_id=1, source_target_pairs={{0,16},{4,20},{8,24},{12,28},{16,0},{20,4},{24,8},{28,12},{1,17},{... | collective-permute-start | bytes 73736 | tf_op jit(solution)/shard_map/ppermute | solution.py:261
  270.3 5.9 %collective-permute-start.14 = (bf16[384,768]{1,0:T(8,128)(2,1)}, bf16[384,768]{1,0:T(8,128)(2,1)S(1)}, u32[]{:S(2)}, u32[]{:S(2)}) collective-permute-start(bf16[384,768]{1,0:T(8,128)(2,1)} %constant_dynamic-slice_fusion.26), channel_id=1, source_target_pairs={{0,1},{1,0},{2,3},{3,2},{4,5},{5,4},{6,7},{7,6},{8,9},{9,8},{10,11... | collective-permute-start | bytes 1769480 | tf_op jit(solution)/shard_map/ppermute | solution.py:261
  276.3 91.7 %collective-permute-start.69 = (bf16[768,768]{1,0:T(8,128)(2,1)S(1)}, bf16[768,768]{1,0:T(8,128)(2,1)S(1)}, u32[]{:S(2)}, u32[]{:S(2)}) collective-permute-start(bf16[768,768]{1,0:T(8,128)(2,1)S(1)} %copy-done.76), channel_id=1, source_target_pairs={{0,1},{1,0},{2,3},{3,2},{4,5},{5,4},{6,7},{7,6},{8,9},{9,8},{10,11... | collective-permute-start | bytes 3538952 | tf_op jit(solution)/shard_map/ppermute | solution.py:261
  276.7 25.8 %collective-permute-start.35 = (bf16[192,768]{1,0:T(8,128)(2,1)S(1)}, bf16[192,768]{1,0:T(8,128)(2,1)S(1)}, u32[]{:S(2)}, u32[]{:S(2)}) collective-permute-start(bf16[192,768]{1,0:T(8,128)(2,1)S(1)} %constant_dynamic-slice_fusion.15), channel_id=1, source_target_pairs={{0,2},{1,3},{2,0},{3,1},{4,6},{5,7},{6,4},{7,5},{8,10},{9,11},{10,... | collective-permute-start | bytes 884744 | tf_op jit(solution)/shard_map/ppermute | solution.py:261
  278.3 14.1 %collective-permute-start.15 = (bf16[192,768]{1,0:T(8,128)(2,1)S(1)}, bf16[192,768]{1,0:T(8,128)(2,1)S(1)}, u32[]{:S(2)}, u32[]{:S(2)}) collective-permute-start(bf16[192,768]{1,0:T(8,128)(2,1)S(1)} %constant_dynamic-slice_fusion.25), channel_id=1, source_target_pairs={{0,2},{1,3},{2,0},{3,1},{4,6},{5,7},{6,4},{7,5},{8,10},{9,11},{10,... | collective-permute-start | bytes 884744 | tf_op jit(solution)/shard_map/ppermute | solution.py:261
  292.4 8.5 %collective-permute-start.45 = (bf16[192,768]{1,0:T(8,128)(2,1)S(1)}, bf16[192,768]{1,0:T(8,128)(2,1)S(1)}, u32[]{:S(2)}, u32[]{:S(2)}) collective-permute-start(bf16[192,768]{1,0:T(8,128)(2,1)S(1)} %constant_dynamic-slice_fusion.10), channel_id=1, source_target_pairs={{0,2},{1,3},{2,0},{3,1},{4,6},{5,7},{6,4},{7,5},{8,10},{9,11},{10,... | collective-permute-start | bytes 884744 | tf_op jit(solution)/shard_map/ppermute | solution.py:261
  300.8 7.6 %collective-permute-start.25 = (bf16[192,768]{1,0:T(8,128)(2,1)S(1)}, bf16[192,768]{1,0:T(8,128)(2,1)S(1)}, u32[]{:S(2)}, u32[]{:S(2)}) collective-permute-start(bf16[192,768]{1,0:T(8,128)(2,1)S(1)} %constant_dynamic-slice_fusion.20), channel_id=1, source_target_pairs={{0,8},{4,12},{8,0},{12,4},{16,24},{20,28},{24,16},{28,20},{1,9},{5... | collective-permute-start | bytes 884744 | tf_op jit(solution)/shard_map/ppermute | solution.py:261
  302.5 68.5 %collective-permute-start.60 = (bf16[768,768]{1,0:T(8,128)(2,1)S(1)}, bf16[768,768]{1,0:T(8,128)(2,1)S(1)}, u32[]{:S(2)}, u32[]{:S(2)}) collective-permute-start(bf16[768,768]{1,0:T(8,128)(2,1)S(1)} %copy-done.75), channel_id=1, source_target_pairs={{0,1},{1,0},{2,3},{3,2},{4,5},{5,4},{6,7},{7,6},{8,9},{9,8},{10,11... | collective-permute-start | bytes 3538952 | tf_op jit(solution)/shard_map/ppermute | solution.py:261
  308.4 6.0 %collective-permute-start.16 = (bf16[96,768]{1,0:T(8,128)(2,1)S(1)}, bf16[96,768]{1,0:T(8,128)(2,1)S(1)}, u32[]{:S(2)}, u32[]{:S(2)}) collective-permute-start(bf16[96,768]{1,0:T(8,128)(2,1)S(1)} %constant_dynamic-slice_fusion.24), channel_id=1, source_target_pairs={{0,4},{4,0},{8,12},{12,8},{16,20},{20,16},{24,28},{28,24},{1,5},{5... | collective-permute-start | bytes 442376 | tf_op jit(solution)/shard_map/ppermute | solution.py:261
  314.4 5.1 collective-permute-start.46
  319.6 6.3 %collective-permute-start.36 = (bf16[96,768]{1,0:T(8,128)(2,1)S(1)}, bf16[96,768]{1,0:T(8,128)(2,1)S(1)}, u32[]{:S(2)}, u32[]{:S(2)}) collective-permute-start(bf16[96,768]{1,0:T(8,128)(2,1)S(1)} %constant_dynamic-slice_fusion.14), channel_id=1, source_target_pairs={{0,8},{4,12},{8,0},{12,4},{16,24},{20,28},{24,16},{28,20},{1,9},{5... | collective-permute-start | bytes 442376 | tf_op jit(solution)/shard_map/ppermute | solution.py:261
  325.9 7.4 %collective-permute-start.26 = (bf16[96,768]{1,0:T(8,128)(2,1)S(1)}, bf16[96,768]{1,0:T(8,128)(2,1)S(1)}, u32[]{:S(2)}, u32[]{:S(2)}) collective-permute-start(bf16[96,768]{1,0:T(8,128)(2,1)S(1)} %constant_dynamic-slice_fusion.19), channel_id=1, source_target_pairs={{0,16},{4,20},{8,24},{12,28},{16,0},{20,4},{24,8},{28,12},{1,17},{... | collective-permute-start | bytes 442376 | tf_op jit(solution)/shard_map/ppermute | solution.py:261
  333.3 4.4 collective-permute-start.17
  342.1 5.5 %collective-permute-start.37 = (bf16[48,768]{1,0:T(8,128)(2,1)S(1)}, bf16[48,768]{1,0:T(8,128)(2,1)S(1)}, u32[]{:S(2)}, u32[]{:S(2)}) collective-permute-start(bf16[48,768]{1,0:T(8,128)(2,1)S(1)} %constant_dynamic-slice_fusion.13), channel_id=1, source_target_pairs={{0,16},{4,20},{8,24},{12,28},{16,0},{20,4},{24,8},{28,12},{1,17},{... | collective-permute-start | bytes 221192 | tf_op jit(solution)/shard_map/ppermute | solution.py:261
  348.9 4.9 collective-permute-start.18
  353.7 4.9 collective-permute-start.48
  366.5 6.5 %collective-permute-start.39 = (bf16[24,768]{1,0:T(8,128)(2,1)S(1)}, bf16[24,768]{1,0:T(8,128)(2,1)S(1)}, u32[]{:S(2)}, u32[]{:S(2)}) collective-permute-start(bf16[24,768]{1,0:T(8,128)(2,1)S(1)} %add_convert_fusion.28), channel_id=1, source_target_pairs={{0,4},{4,0},{8,12},{12,8},{16,20},{20,16},{24,28},{28,24},{1,5},{5... | collective-permute-start | bytes 110600 | tf_op jit(solution)/shard_map/ppermute | solution.py:261
  368.0 8.0 %collective-permute-start.29 = (bf16[24,768]{1,0:T(8,128)(2,1)S(1)}, bf16[24,768]{1,0:T(8,128)(2,1)S(1)}, u32[]{:S(2)}, u32[]{:S(2)}) collective-permute-start(bf16[24,768]{1,0:T(8,128)(2,1)S(1)} %add_convert_fusion.29), channel_id=1, source_target_pairs={{0,2},{1,3},{2,0},{3,1},{4,6},{5,7},{6,4},{7,5},{8,10},{9,11},{10,... | collective-permute-start | bytes 110600 | tf_op jit(solution)/shard_map/ppermute | solution.py:261
  371.1 5.8 %collective-permute-start.19 = (bf16[24,768]{1,0:T(8,128)(2,1)S(1)}, bf16[24,768]{1,0:T(8,128)(2,1)S(1)}, u32[]{:S(2)}, u32[]{:S(2)}) collective-permute-start(bf16[24,768]{1,0:T(8,128)(2,1)S(1)} %add_convert_fusion.30), channel_id=1, source_target_pairs={{0,16},{4,20},{8,24},{12,28},{16,0},{20,4},{24,8},{28,12},{1,17},{... | collective-permute-start | bytes 110600 | tf_op jit(solution)/shard_map/ppermute | solution.py:261
  373.0 4.9 collective-permute-start.49
  376.0 61.1 %collective-permute-start.70 = (bf16[768,768]{1,0:T(8,128)(2,1)S(1)}, bf16[768,768]{1,0:T(8,128)(2,1)S(1)}, u32[]{:S(2)}, u32[]{:S(2)}) collective-permute-start(bf16[768,768]{1,0:T(8,128)(2,1)S(1)} %add_convert_fusion.2), channel_id=1, source_target_pairs={{0,2},{1,3},{2,0},{3,1},{4,6},{5,7},{6,4},{7,5},{8,10},{9,11},{10,... | collective-permute-start | bytes 3538952 | tf_op jit(solution)/shard_map/ppermute | solution.py:261
  376.9 5.6 %collective-permute-start.40 = (bf16[48,768]{1,0:T(8,128)(2,1)S(1)}, bf16[48,768]{1,0:T(8,128)(2,1)S(1)}, u32[]{:S(2)}, u32[]{:S(2)}) collective-permute-start(bf16[48,768]{1,0:T(8,128)(2,1)S(1)} %pad_maximum_fusion.18), channel_id=1, source_target_pairs={{0,16},{4,20},{8,24},{12,28},{16,0},{20,4},{24,8},{28,12},{1,17},{... | collective-permute-start | bytes 221192 | tf_op jit(solution)/shard_map/ppermute | solution.py:261
  377.9 4.7 collective-permute-start.30
  382.5 6.6 %collective-permute-start.20 = (bf16[48,768]{1,0:T(8,128)(2,1)S(1)}, bf16[48,768]{1,0:T(8,128)(2,1)S(1)}, u32[]{:S(2)}, u32[]{:S(2)}) collective-permute-start(bf16[48,768]{1,0:T(8,128)(2,1)S(1)} %pad_maximum_fusion.16), channel_id=1, source_target_pairs={{0,8},{4,12},{8,0},{12,4},{16,24},{20,28},{24,16},{28,20},{1,9},{5... | collective-permute-start | bytes 221192 | tf_op jit(solution)/shard_map/ppermute | solution.py:261
  382.6 7.8 %collective-permute-start.50 = (bf16[48,768]{1,0:T(8,128)(2,1)S(1)}, bf16[48,768]{1,0:T(8,128)(2,1)S(1)}, u32[]{:S(2)}, u32[]{:S(2)}) collective-permute-start(bf16[48,768]{1,0:T(8,128)(2,1)S(1)} %pad_maximum_fusion.19), channel_id=1, source_target_pairs={{0,8},{4,12},{8,0},{12,4},{16,24},{20,28},{24,16},{28,20},{1,9},{5... | collective-permute-start | bytes 221192 | tf_op jit(solution)/shard_map/ppermute | solution.py:261
  389.2 5.1 collective-permute-start.41
  390.4 7.6 %collective-permute-start.31 = (bf16[96,768]{1,0:T(8,128)(2,1)S(1)}, bf16[96,768]{1,0:T(8,128)(2,1)S(1)}, u32[]{:S(2)}, u32[]{:S(2)}) collective-permute-start(bf16[96,768]{1,0:T(8,128)(2,1)S(1)} %pad_maximum_fusion.13), channel_id=1, source_target_pairs={{0,16},{4,20},{8,24},{12,28},{16,0},{20,4},{24,8},{28,12},{1,17},{... | collective-permute-start | bytes 442376 | tf_op jit(solution)/shard_map/ppermute | solution.py:261
  394.3 5.1 collective-permute-start.21
  398.0 5.1 collective-permute-start.51
  399.5 8.3 %collective-permute-start.42 = (bf16[192,768]{1,0:T(8,128)(2,1)S(1)}, bf16[192,768]{1,0:T(8,128)(2,1)S(1)}, u32[]{:S(2)}, u32[]{:S(2)}) collective-permute-start(bf16[192,768]{1,0:T(8,128)(2,1)S(1)} %pad_maximum_fusion.8), channel_id=1, source_target_pairs={{0,2},{1,3},{2,0},{3,1},{4,6},{5,7},{6,4},{7,5},{8,10},{9,11},{10,... | collective-permute-start | bytes 884744 | tf_op jit(solution)/shard_map/ppermute | solution.py:261
  403.1 6.7 %collective-permute-start.32 = (bf16[192,768]{1,0:T(8,128)(2,1)S(1)}, bf16[192,768]{1,0:T(8,128)(2,1)S(1)}, u32[]{:S(2)}, u32[]{:S(2)}) collective-permute-start(bf16[192,768]{1,0:T(8,128)(2,1)S(1)} %pad_maximum_fusion.7), channel_id=1, source_target_pairs={{0,8},{4,12},{8,0},{12,4},{16,24},{20,28},{24,16},{28,20},{1,9},{5... | collective-permute-start | bytes 884744 | tf_op jit(solution)/shard_map/ppermute | solution.py:261
  407.8 7.9 %collective-permute-start.22 = (bf16[192,768]{1,0:T(8,128)(2,1)S(1)}, bf16[192,768]{1,0:T(8,128)(2,1)S(1)}, u32[]{:S(2)}, u32[]{:S(2)}) collective-permute-start(bf16[192,768]{1,0:T(8,128)(2,1)S(1)} %pad_maximum_fusion.6), channel_id=1, source_target_pairs={{0,2},{1,3},{2,0},{3,1},{4,6},{5,7},{6,4},{7,5},{8,10},{9,11},{10,... | collective-permute-start | bytes 884744 | tf_op jit(solution)/shard_map/ppermute | solution.py:261
  409.8 9.0 %collective-permute-start.52 = (bf16[192,768]{1,0:T(8,128)(2,1)S(1)}, bf16[192,768]{1,0:T(8,128)(2,1)S(1)}, u32[]{:S(2)}, u32[]{:S(2)}) collective-permute-start(bf16[192,768]{1,0:T(8,128)(2,1)S(1)} %pad_maximum_fusion.9), channel_id=1, source_target_pairs={{0,2},{1,3},{2,0},{3,1},{4,6},{5,7},{6,4},{7,5},{8,10},{9,11},{10,... | collective-permute-start | bytes 884744 | tf_op jit(solution)/shard_map/ppermute | solution.py:261
  419.0 28.4 %collective-permute-start.61 = (bf16[768,768]{1,0:T(8,128)(2,1)S(1)}, bf16[768,768]{1,0:T(8,128)(2,1)S(1)}, u32[]{:S(2)}, u32[]{:S(2)}) collective-permute-start(bf16[768,768]{1,0:T(8,128)(2,1)S(1)} %add_convert_fusion.4), channel_id=1, source_target_pairs={{0,2},{1,3},{2,0},{3,1},{4,6},{5,7},{6,4},{7,5},{8,10},{9,11},{10,... | collective-permute-start | bytes 3538952 | tf_op jit(solution)/shard_map/ppermute | solution.py:261
  420.8 15.4 %collective-permute-start.33 = (bf16[384,768]{1,0:T(8,128)(2,1)S(1)}, bf16[384,768]{1,0:T(8,128)(2,1)S(1)}, u32[]{:S(2)}, u32[]{:S(2)}) collective-permute-start(bf16[384,768]{1,0:T(8,128)(2,1)S(1)} %pad_maximum_fusion.1), channel_id=1, source_target_pairs={{0,4},{4,0},{8,12},{12,8},{16,20},{20,16},{24,28},{28,24},{1,5},{5... | collective-permute-start | bytes 1769480 | tf_op jit(solution)/shard_map/ppermute | solution.py:261
  436.2 70.3 %collective-permute-start.53 = (bf16[384,768]{1,0:T(8,128)(2,1)S(1)}, bf16[384,768]{1,0:T(8,128)(2,1)S(1)}, u32[]{:S(2)}, u32[]{:S(2)}) collective-permute-start(bf16[384,768]{1,0:T(8,128)(2,1)S(1)} %pad_maximum_fusion.3), channel_id=1, source_target_pairs={{0,1},{1,0},{2,3},{3,2},{4,5},{5,4},{6,7},{7,6},{8,9},{9,8},{10,11... | collective-permute-start | bytes 1769480 | tf_op jit(solution)/shard_map/ppermute | solution.py:261
  441.4 15.8 %collective-permute-start.71 = (bf16[384,768]{1,0:T(8,128)(2,1)S(1)}, bf16[384,768]{1,0:T(8,128)(2,1)S(1)}, u32[]{:S(2)}, u32[]{:S(2)}) collective-permute-start(bf16[384,768]{1,0:T(8,128)(2,1)S(1)} %constant_dynamic-slice_fusion.2), channel_id=1, source_target_pairs={{0,4},{4,0},{8,12},{12,8},{16,20},{20,16},{24,28},{28,24},{1,5},{5... | collective-permute-start | bytes 1769480 | tf_op jit(solution)/shard_map/ppermute | solution.py:261
  449.3 16.3 %collective-permute-start.62 = (bf16[384,768]{1,0:T(8,128)(2,1)S(1)}, bf16[384,768]{1,0:T(8,128)(2,1)S(1)}, u32[]{:S(2)}, u32[]{:S(2)}) collective-permute-start(bf16[384,768]{1,0:T(8,128)(2,1)S(1)} %constant_dynamic-slice_fusion.6), channel_id=1, source_target_pairs={{0,8},{4,12},{8,0},{12,4},{16,24},{20,28},{24,16},{28,20},{1,9},{5... | collective-permute-start | bytes 1769480 | tf_op jit(solution)/shard_map/ppermute | solution.py:261
  457.4 16.2 %collective-permute-start.72 = (bf16[192,768]{1,0:T(8,128)(2,1)S(1)}, bf16[192,768]{1,0:T(8,128)(2,1)S(1)}, u32[]{:S(2)}, u32[]{:S(2)}) collective-permute-start(bf16[192,768]{1,0:T(8,128)(2,1)S(1)} %constant_dynamic-slice_fusion.1), channel_id=1, source_target_pairs={{0,8},{4,12},{8,0},{12,4},{16,24},{20,28},{24,16},{28,20},{1,9},{5... | collective-permute-start | bytes 884744 | tf_op jit(solution)/shard_map/ppermute | solution.py:261
  465.8 18.6 %collective-permute-start.63 = (bf16[192,768]{1,0:T(8,128)(2,1)S(1)}, bf16[192,768]{1,0:T(8,128)(2,1)S(1)}, u32[]{:S(2)}, u32[]{:S(2)}) collective-permute-start(bf16[192,768]{1,0:T(8,128)(2,1)S(1)} %constant_dynamic-slice_fusion.5), channel_id=1, source_target_pairs={{0,16},{4,20},{8,24},{12,28},{16,0},{20,4},{24,8},{28,12},{1,17},{... | collective-permute-start | bytes 884744 | tf_op jit(solution)/shard_map/ppermute | solution.py:261
  473.7 12.2 %collective-permute-start.73 = (bf16[96,768]{1,0:T(8,128)(2,1)S(1)}, bf16[96,768]{1,0:T(8,128)(2,1)S(1)}, u32[]{:S(2)}, u32[]{:S(2)}) collective-permute-start(bf16[96,768]{1,0:T(8,128)(2,1)S(1)} %constant_dynamic-slice_fusion), channel_id=1, source_target_pairs={{0,16},{4,20},{8,24},{12,28},{16,0},{20,4},{24,8},{28,12},{1,17},{... | collective-permute-start | bytes 442376 | tf_op jit(solution)/shard_map/ppermute | solution.py:261
  484.4 6.0 %collective-permute-start.64 = (bf16[96,768]{1,0:T(8,128)(2,1)S(1)}, bf16[96,768]{1,0:T(8,128)(2,1)S(1)}, u32[]{:S(2)}, u32[]{:S(2)}) collective-permute-start(bf16[96,768]{1,0:T(8,128)(2,1)S(1)} %constant_dynamic-slice_fusion.4), channel_id=1, source_target_pairs={{0,4},{4,0},{8,12},{12,8},{16,20},{20,16},{24,28},{28,24},{1,5},{5... | collective-permute-start | bytes 442376 | tf_op jit(solution)/shard_map/ppermute | solution.py:261
  485.9 7.0 %collective-permute-start.74 = (bf16[96,768]{1,0:T(8,128)(2,1)S(1)}, bf16[96,768]{1,0:T(8,128)(2,1)S(1)}, u32[]{:S(2)}, u32[]{:S(2)}) collective-permute-start(bf16[96,768]{1,0:T(8,128)(2,1)S(1)} %add_convert_fusion.17), channel_id=1, source_target_pairs={{0,16},{4,20},{8,24},{12,28},{16,0},{20,4},{24,8},{28,12},{1,17},{... | collective-permute-start | bytes 442376 | tf_op jit(solution)/shard_map/ppermute | solution.py:261
  490.5 5.2 collective-permute-start.65
  493.0 12.6 %collective-permute-start.75 = (bf16[192,768]{1,0:T(8,128)(2,1)S(1)}, bf16[192,768]{1,0:T(8,128)(2,1)S(1)}, u32[]{:S(2)}, u32[]{:S(2)}) collective-permute-start(bf16[192,768]{1,0:T(8,128)(2,1)S(1)} %pad_maximum_fusion.11), channel_id=1, source_target_pairs={{0,8},{4,12},{8,0},{12,4},{16,24},{20,28},{24,16},{28,20},{1,9},{5... | collective-permute-start | bytes 884744 | tf_op jit(solution)/shard_map/ppermute | solution.py:261
  495.7 13.1 %collective-permute-start.66 = (bf16[192,768]{1,0:T(8,128)(2,1)S(1)}, bf16[192,768]{1,0:T(8,128)(2,1)}, u32[]{:S(2)}, u32[]{:S(2)}) collective-permute-start(bf16[192,768]{1,0:T(8,128)(2,1)S(1)} %pad_maximum_fusion.10), channel_id=1, source_target_pairs={{0,16},{4,20},{8,24},{12,28},{16,0},{20,4},{24,8},{28,12},{1,17},{... | collective-permute-start | bytes 884744 | tf_op jit(solution)/shard_map/ppermute | solution.py:261
  506.5 14.4 %collective-permute-start.76 = (bf16[384,768]{1,0:T(8,128)(2,1)}, bf16[384,768]{1,0:T(8,128)(2,1)S(1)}, u32[]{:S(2)}, u32[]{:S(2)}) collective-permute-start(bf16[384,768]{1,0:T(8,128)(2,1)} %pad_maximum_fusion.5), channel_id=1, source_target_pairs={{0,4},{4,0},{8,12},{12,8},{16,20},{20,16},{24,28},{28,24},{1,5},{5... | collective-permute-start | bytes 1769480 | tf_op jit(solution)/shard_map/ppermute | solution.py:261
  510.7 13.8 %collective-permute-start.67 = (bf16[384,768]{1,0:T(8,128)(2,1)}, bf16[384,768]{1,0:T(8,128)(2,1)}, u32[]{:S(2)}, u32[]{:S(2)}) collective-permute-start(bf16[384,768]{1,0:T(8,128)(2,1)} %pad_maximum_fusion.4), channel_id=1, source_target_pairs={{0,8},{4,12},{8,0},{12,4},{16,24},{20,28},{24,16},{28,20},{1,9},{5... | collective-permute-start | bytes 1769480 | tf_op jit(solution)/shard_map/ppermute | solution.py:261
  (99 other events, 599.5 us)
